TPU v7x, 32 devices: a whole 2x2x4 slice. The times are simulated.
32 devices in a mesh: dp: 16 (over z, y, core), mp: 2 (over x).
Axes of the slice: x: 2, y: 2, z: 4, core: 2. Of those that a mesh axis runs over, the one named last changes fastest.
Arguments:
- dino_tokens: bfloat16 [8192, 1024], P('dp', 'mp'), may hold values from -6 to 6
- siglip_tokens: bfloat16 [8192, 1152], P('dp', 'mp'), may hold values from -6 to 6
- dino_norm_one: float32 [1024], replicated, may hold values from 0.25 to 1.75
- dino_qkv: bfloat16 [1024, 3, 1024], P('dp', None, 'mp'), may hold values from -6.05625 to 6.05625
- dino_out: bfloat16 [1024, 1024], P('mp', 'dp'), may hold values from -0.1875 to 0.1875
- dino_norm_two: float32 [1024], replicated, may hold values from 0.25 to 1.75
- dino_up: bfloat16 [1024, 4096], P('dp', 'mp'), may hold values from -0.1875 to 0.1875
- dino_down: bfloat16 [4096, 1024], P('mp', 'dp'), may hold values from -0.09375 to 0.09375
- siglip_norm_one: float32 [1152], replicated, may hold values from 0.25 to 1.75
- siglip_qkv: bfloat16 [1152, 3, 1152], P('dp', None, 'mp'), may hold values from -5.709887 to 5.709887
- siglip_out: bfloat16 [1152, 1152], P('mp', 'dp'), may hold values from -0.1875 to 0.1875
- siglip_norm_two: float32 [1152], replicated, may hold values from 0.25 to 1.75
- siglip_up: bfloat16 [1152, 4304], P('dp', 'mp'), may hold values from -0.1875 to 0.1875
- siglip_down: bfloat16 [4304, 1152], P('mp', 'dp'), may hold values from -0.09375 to 0.09375
Outputs:
- dino_result: bfloat16 [8192, 1024], P('dp', 'mp')
- siglip_result: bfloat16 [8192, 1152], P('dp', 'mp')
All inputs are finite; a program needn't handle non-finite values.
Results may differ from a plain program's by a relative error of at most 0.012.
Values may be sent and summed in bfloat16 or wider, within the bound.
No kernel may reach another device: no remote copies, remote signals or barrier semaphores. Data moves between devices by JAX's collectives and lax.ppermute only.
A program may use at most 128 MiB of HBM per device.

v0:
```python
import functools
import math

import jax
import jax.numpy as jnp
import numpy as np
from jax import lax
from jax.experimental import pallas as pl
from jax.experimental.pallas import tpu as pltpu
from jax.sharding import PartitionSpec as P


HEADS = 16
PATCHES = 256
EPS = 1e-06
LANES = 128
BLOCK = 256
BF16 = jnp.bfloat16
F32 = jnp.float32
MLP_VMEM = 24 * 2**20
NT = (((1,), (1,)), ((), ()))


def dot(a, b):
    return jnp.dot(a, b, preferred_element_type=F32)


def dot_nt(a, b):
    return lax.dot_general(a, b, NT, preferred_element_type=F32)


def gelu(x, approx):
    if approx:
        inner = math.sqrt(2.0 / math.pi) * (x + 0.044715 * (x * x * x))
        return 0.5 * x * (1.0 + jnp.tanh(inner))
    return 0.5 * x * (1.0 + lax.erf(x * math.sqrt(0.5)))


def layer_norm(values, gain):
    values = values.astype(F32)
    center = values - jnp.mean(values, axis=-1, keepdims=True)
    spread = jnp.mean(center * center, axis=-1, keepdims=True)
    return (center * lax.rsqrt(spread + EPS) * gain).astype(BF16)


def pack_attention(qkv, out):
    local = qkv.shape[2]
    main = local // LANES * LANES
    parts = [qkv[:, 0], qkv[:, 1], qkv[:, 2], out.T]
    packed = [p[:, :main] for p in parts]
    if main < local:
        packed[3:3] = [p[:, main:] for p in parts]
    return jnp.concatenate(packed, axis=1)


def project_kernel(count, local, turned, table, own_ref, other_ref, gain_ref, *rest):
    weights = rest[:count]
    weight, whole, projected, normed, sems = rest[count:]
    main = local // LANES * LANES
    extra = local - main
    part = weights[0].shape[0]

    def copy(at):
        start = pl.multiple_of(table[at] * part, 8)
        return pltpu.make_async_copy(
            weights[at], weight.at[pl.ds(start, part), :], sems.at[at]
        )

    for at in range(count):
        copy(at).start()
    rows = whole.shape[0]
    first = lax.axis_index("mp") == 0

    def load(ref, at):
        if not turned:
            return ref[pl.ds(at, PATCHES), :].astype(F32)
        values = ref[:, pl.ds(at, PATCHES)].astype(F32)
        half = values.shape[0]
        spare = -half % LANES
        if spare:
            values = jnp.concatenate([values, jnp.zeros((spare, PATCHES), F32)], axis=0)
        return values.T[:, :half]

    def norm_frame(f, _):
        at = pl.multiple_of(f * PATCHES, PATCHES)
        own, other = load(own_ref, at), load(other_ref, at)
        halves = [jnp.where(first, own, other), jnp.where(first, other, own)]
        values = jnp.concatenate(halves, axis=1)
        whole[pl.ds(at, PATCHES), :] = values.astype(BF16)
        normed[pl.ds(at, PATCHES), :] = layer_norm(values, gain_ref[...])
        return 0

    lax.fori_loop(0, rows // PATCHES, norm_frame, 0)
    for at in range(count):
        copy(at).wait()

    columns = 3 * main + (2 * LANES if extra else 0)
    step = 2 * BLOCK
    for lo in range(0, columns, step):
        size = min(step, columns - lo)
        piece = dot(normed[...], weight[:, lo : lo + size])
        projected[:, lo : lo + size] = piece.astype(BF16)


def attend_kernel(local, heads, weight, whole, projected, mine_ref, send_ref, context):
    main = local // LANES * LANES
    extra = local - main
    head = local // heads
    rows = whole.shape[0]

    def frame(f, _):
        at = pl.multiple_of(f * PATCHES, PATCHES)

        def tile(column):
            return projected[pl.ds(at, PATCHES), column : column + LANES]

        tiles = [[tile(j * main + t * LANES) for t in range(main // LANES)] for j in range(3)]
        if extra:
            left = tile(3 * main)
            tiles[0].append(left)
            turned = pltpu.roll(left.astype(F32), LANES - extra, 1)
            tiles[1].append(turned.astype(BF16))
            tiles[2].append(tile(3 * main + LANES))
        lane = lax.broadcasted_iota(jnp.int32, (PATCHES, LANES), 1)
        context_tiles = [None] * len(tiles[0])
        for h in range(heads):
            lo, hi = h * head, (h + 1) * head
            used = list(range(lo // LANES, (hi - 1) // LANES + 1))
            masks = [(lane >= lo - t * LANES) & (lane < hi - t * LANES) for t in used]
            query = [
                jnp.where(mask, tiles[0][t], jnp.zeros_like(tiles[0][t]))
                for t, mask in zip(used, masks)
            ]
            keys = [tiles[1][t] for t in used]
            values = [tiles[2][t] for t in used]
            cat = lambda xs: xs[0] if len(xs) == 1 else jnp.concatenate(xs, axis=1)
            scores = dot_nt(cat(query), cat(keys))
            top = jnp.max(scores, axis=-1, keepdims=True)
            expo = jnp.exp((scores - top) * (1.0 / math.sqrt(head)))
            share = 1.0 / jnp.sum(expo, axis=-1, keepdims=True)
            mixed = dot(expo.astype(BF16), cat(values)) * share
            for k, (t, mask) in enumerate(zip(used, masks)):
                now = mixed[:, k * LANES : (k + 1) * LANES]
                before = jnp.zeros_like(now) if context_tiles[t] is None else context_tiles[t]
                context_tiles[t] = jnp.where(mask, now, before)
        first = 0
        if extra:
            last = pltpu.roll(context_tiles.pop(), LANES - extra, 1)
            context[pl.ds(at, PATCHES), :LANES] = last.astype(BF16)
            first = LANES
        for t, piece in enumerate(context_tiles):
            lo = first + t * LANES
            context[pl.ds(at, PATCHES), lo : lo + LANES] = piece.astype(BF16)
        return 0

    lax.fori_loop(0, rows // PATCHES, frame, 0)
    lo = 3 * main + (LANES if extra else 0)
    size = main + (LANES if extra else 0)
    total = dot_nt(context[...], weight[:, lo : lo + size])
    send_ref[...] = total.astype(BF16)
    mine_ref[...] = total + whole[...].astype(F32)


def project(own, other, gain, weights, table, local, turned):
    rows, half = own.shape[::-1] if turned else own.shape
    width = 2 * half
    columns = weights[0].shape[1]
    count = len(weights)
    main = local // LANES * LANES
    extra = LANES if main < local else 0
    vmem = pl.BlockSpec(memory_space=pltpu.VMEM)
    anyspace = pl.BlockSpec(memory_space=pl.ANY)
    return pl.pallas_call(
        functools.partial(project_kernel, count, local, turned),
        out_shape=(
            pltpu.VMEM((width, columns), BF16),
            pltpu.VMEM((rows, width), BF16),
            pltpu.VMEM((rows, 3 * main + extra * 2), BF16),
        ),
        grid_spec=pltpu.PrefetchScalarGridSpec(
            num_scalar_prefetch=1,
            grid=(),
            in_specs=[vmem] * 3 + [anyspace] * count,
            out_specs=(vmem,) * 3,
            scratch_shapes=[
                pltpu.VMEM((rows, width), BF16),
                pltpu.SemaphoreType.DMA((count,)),
            ],
        ),
        compiler_params=pltpu.CompilerParams(vmem_limit_bytes=MLP_VMEM),
    )(table, own, other, gain.reshape(1, width), *weights)


def attention(weight, whole, projected, local, heads):
    rows, width = whole.shape
    size = -(-local // LANES) * LANES
    vmem = pl.BlockSpec(memory_space=pltpu.VMEM)
    return pl.pallas_call(
        functools.partial(attend_kernel, local, heads),
        out_shape=(
            jax.ShapeDtypeStruct((rows, width), F32),
            jax.ShapeDtypeStruct((rows, width), BF16),
        ),
        in_specs=[vmem] * 3,
        out_specs=(vmem, vmem),
        scratch_shapes=[pltpu.VMEM((rows, size), BF16)],
        compiler_params=pltpu.CompilerParams(vmem_limit_bytes=MLP_VMEM),
    )(weight, whole, projected)


def middle_kernel(turned, mine_ref, got_ref, gain_ref, second_ref, mid_ref):
    rows = mine_ref.shape[0]
    half = mine_ref.shape[1] // 2
    first = lax.axis_index("mp") == 0
    for at in range(0, rows, PATCHES):
        span = slice(at, at + PATCHES)
        total = mine_ref[span, :] + got_ref[span, :].astype(F32)
        middle = total.astype(BF16).astype(F32)
        second_ref[span, :] = layer_norm(middle, gain_ref[...])
        own = jnp.where(first, middle[:, :half], middle[:, half:])
        if turned:
            spare = -half % LANES
            if spare:
                own = jnp.concatenate([own, jnp.zeros((PATCHES, spare), F32)], axis=1)
            mid_ref[:, span] = own.T[:half, :].astype(BF16)
        else:
            mid_ref[span, :] = own.astype(BF16)


def middle(mine, got, gain, turned):
    rows, width = mine.shape
    half = width // 2
    vmem = pl.BlockSpec(memory_space=pltpu.VMEM)
    return pl.pallas_call(
        functools.partial(middle_kernel, turned),
        out_shape=(
            jax.ShapeDtypeStruct((rows, width), BF16),
            jax.ShapeDtypeStruct((half, rows) if turned else (rows, half), BF16),
        ),
        in_specs=[vmem] * 3,
        out_specs=(vmem, vmem),
        compiler_params=pltpu.CompilerParams(vmem_limit_bytes=MLP_VMEM),
    )(mine, got, gain.reshape(1, width))


def pack_mlp(up, down):
    spare = -up.shape[1] % LANES
    both = jnp.concatenate([up, down.T], axis=0)
    return jnp.pad(both, ((0, 0), (0, spare))) if spare else both


def weight_copies(table, sources, first, targets, sems):
    r = targets[0].shape[1]
    return [
        [
            pltpu.make_async_copy(
                source.at[pl.ds(k * r, r), :],
                target.at[table[first + i]],
                sems.at[k * len(sources) + i],
            )
            for i, source in enumerate(sources)
        ]
        for k, target in enumerate(targets)
    ]


def load_kernel(count, table, *refs):
    up, down, sems = refs[count:]
    copies = sum(weight_copies(table, refs[:count], 0, (up, down), sems), [])
    for c in copies:
        c.start()
    for c in copies:
        c.wait()


def flat(ref):
    return ref.reshape(ref.shape[0] * ref.shape[1], ref.shape[2])


def raise_to(approx, tokens_ref, up_ref, hidden_ref, lo, hi):
    for at in range(lo, hi, 2 * BLOCK):
        end = min(at + 2 * BLOCK, hi)
        raised = dot(tokens_ref[...], up_ref[:, at:end])
        hidden_ref[:, at:end] = gelu(raised, approx).astype(BF16)


def lower(hidden_ref, down, which, turned):
    half = down.shape[0] * down.shape[1] // 2
    at = pl.multiple_of(which * half, 8)
    weight = flat(down)[pl.ds(at, half), :]
    if turned:
        return dot_nt(weight, hidden_ref[...])
    return dot_nt(hidden_ref[...], weight)


def lower_other(hidden_ref, down, sent, send_ref, sem, turned):
    sent[...] = lower(hidden_ref, down, 1 - lax.axis_index("mp"), turned).astype(BF16)
    out = pltpu.make_async_copy(sent, send_ref, sem)
    out.start()
    out.wait()


def mlp_kernel(approx, turned, count, first, table, tokens_ref, *refs):
    sources = refs[2 : 2 + count]
    send_ref, hidden_ref, up, down, sent, sems = refs[2 + count :]
    copies = weight_copies(table, sources, first, (up, down), sems)
    for c in sum(copies, []):
        c.start()
    for c in copies[0]:
        c.wait()
    raise_to(approx, tokens_ref, flat(up), hidden_ref, 0, up.shape[2])
    for c in copies[1]:
        c.wait()
    lower_other(hidden_ref, down, sent, send_ref, sems.at[2 * count], turned)


def finish_kernel(*refs):
    for e in range(2):
        hidden_ref, mid_ref, down = refs[3 * e : 3 * e + 3]
        total = lower(hidden_ref, down, lax.axis_index("mp"), e == 1)
        refs[6 + e][...] = mid_ref[...].astype(F32) + total


def load(weights, table, width):
    r, columns = weights[0].shape[0] // 2, weights[0].shape[1]
    count = len(weights)
    shape = pltpu.VMEM((width // r, r, columns), BF16)
    vmem = pl.BlockSpec(memory_space=pltpu.VMEM)
    anyspace = pl.BlockSpec(memory_space=pl.ANY)
    return pl.pallas_call(
        functools.partial(load_kernel, count),
        out_shape=(shape, shape),
        grid_spec=pltpu.PrefetchScalarGridSpec(
            num_scalar_prefetch=1,
            grid=(),
            in_specs=[anyspace] * count,
            out_specs=(vmem, vmem),
            scratch_shapes=[pltpu.SemaphoreType.DMA((2 * count,))],
        ),
        compiler_params=pltpu.CompilerParams(vmem_limit_bytes=MLP_VMEM),
    )(table, *weights)


def mlp(tokens, loaded, weights, first, table, approx, turned):
    rows, width = tokens.shape
    count = len(weights)
    shape = loaded[0].shape
    sent = (width // 2, rows) if turned else (rows, width // 2)
    vmem = pl.BlockSpec(memory_space=pltpu.VMEM)
    anyspace = pl.BlockSpec(memory_space=pl.ANY)
    send, hidden, _, down = pl.pallas_call(
        functools.partial(mlp_kernel, approx, turned, count, first),
        out_shape=(
            pltpu.HBM(sent, BF16),
            pltpu.VMEM((rows, shape[2]), BF16),
            pltpu.VMEM(shape, BF16),
            pltpu.VMEM(shape, BF16),
        ),
        grid_spec=pltpu.PrefetchScalarGridSpec(
            num_scalar_prefetch=1,
            grid=(),
            in_specs=[vmem] * 3 + [anyspace] * count,
            out_specs=(anyspace, vmem, vmem, vmem),
            scratch_shapes=[
                pltpu.VMEM(sent, BF16),
                pltpu.SemaphoreType.DMA((2 * count + 1,)),
            ],
        ),
        input_output_aliases={2: 2, 3: 3},
        compiler_params=pltpu.CompilerParams(vmem_limit_bytes=MLP_VMEM),
    )(table, tokens, *loaded, *weights)
    return send, hidden, down


def finish(hidden_values, mids, downs):
    vmem = pl.BlockSpec(memory_space=pltpu.VMEM)
    operands = [x for e in range(2) for x in (hidden_values[e], mids[e], downs[e])]
    return pl.pallas_call(
        finish_kernel,
        out_shape=tuple(jax.ShapeDtypeStruct(x.shape, F32) for x in mids),
        in_specs=[vmem] * 6,
        out_specs=(vmem, vmem),
        compiler_params=pltpu.CompilerParams(vmem_limit_bytes=MLP_VMEM),
        name="finish",
    )(*operands)


def swap_mp(x):
    return lax.ppermute(x, "mp", [(0, 1), (1, 0)])


def ring_order(chips):
    return [0] + list(range(1, chips, 2)) + list(range(chips - 2, 0, -2))


class Ring:
    def __init__(self, n):
        chips = n // 2
        order = ring_order(chips)
        after = {order[i]: order[(i + 1) % chips] for i in range(chips)}
        before = {v: k for k, v in after.items()}
        self.hop = [(2 * c, 2 * after[c]) for c in range(chips)]
        self.hop += [(2 * c + 1, 2 * before[c] + 1) for c in range(chips)]
        self.core = [(d, d ^ 1) for d in range(n)]
        self.hops = chips - 1
        source = {b: a for a, b in self.hop}
        owners = list(range(n))
        self.tables = []
        for _ in range(chips):
            self.tables += [owners, [owners[d ^ 1] for d in range(n)]]
            owners = [owners[source[d]] for d in range(n)]

    def both(self, x):
        return [x, lax.ppermute(x, "dp", self.core)]

    def step(self, x):
        return lax.ppermute(x, "dp", self.hop)


def local(
    mesh_sizes,
    dino_tokens,
    siglip_tokens,
    dino_norm_one,
    dino_qkv,
    dino_out,
    dino_norm_two,
    dino_up,
    dino_down,
    siglip_norm_one,
    siglip_qkv,
    siglip_out,
    siglip_norm_two,
    siglip_up,
    siglip_down,
):
    n, groups = mesh_sizes
    d = lax.axis_index("dp")
    heads = HEADS // groups
    tokens = [dino_tokens, siglip_tokens.T]
    others = [swap_mp(x) for x in tokens]
    packed = [pack_attention(dino_qkv, dino_out), pack_attention(siglip_qkv, siglip_out)]
    locals_ = [dino_qkv.shape[2], siglip_qkv.shape[2]]
    shards = [pack_mlp(dino_up, dino_down), pack_mlp(siglip_up, siglip_down)]
    direct = direct_ring(n)
    if direct:
        assert all(p.shape[0] % 8 == 0 for p in packed)
    gots, mines = [], []

    def attend(e, weights):
        state = project(tokens[e], others[e], ones[e], weights, table, locals_[e], e == 1)
        mine, send = attention(*state, locals_[e], heads)
        mines.append(mine)
        gots.append(swap_mp(send))

    ones = [dino_norm_one, siglip_norm_one]
    twos = [dino_norm_two, siglip_norm_two]
    if direct:
        ring = Ring(n)
        table = jnp.array(np.array(ring.tables, np.int32).T)
        table = lax.dynamic_index_in_dim(table, d, 0, keepdims=False)
        streams = [packed, shards]
        gathered = []
        for stage, now in enumerate(streams):
            now = list(now)
            gathered.append([ring.both(x) for x in now])
            for h in range(ring.hops):
                if (stage, h) == (0, 2):
                    now[0] = lax.optimization_barrier((now[0], table))[0]
                for e in range(2):
                    now[e] = ring.step(now[e])
                    gathered[-1][e] += ring.both(now[e])
        for e in range(2):
            attend(e, gathered[0][e])
    else:
        table = jnp.zeros((1,), jnp.int32)
        gather = lambda x: lax.all_gather(x, "dp", axis=0, tiled=True)
        for e in range(2):
            attend(e, [gather(packed[e])])
        ups, downs = [dino_up, siglip_up], [dino_down.T, siglip_down.T]
        gathered = [None, [[pack_mlp(gather(u), gather(v).T)] for u, v in zip(ups, downs)]]
    mids, seconds = [], []
    for e in range(2):
        second, mid = middle(mines[e], gots[e], twos[e], e == 1)
        seconds.append(second)
        mids.append(mid)
    sends, hidden_values, downs = [], [], []
    for e in range(2):
        shards = gathered[1][e]
        first = max(len(shards) - 2, 1)
        loaded = load(shards[:first], table, seconds[e].shape[1])
        send, hidden, down = mlp(seconds[e], loaded, shards[first:], first, table, e == 1, e == 1)
        sends.append(swap_mp(send))
        hidden_values.append(hidden)
        downs.append(down)
    mines = finish(hidden_values, mids, downs)
    results = [(mines[e] + sends[e].astype(F32)).astype(BF16) for e in range(2)]
    return results[0], results[1].T


def direct_ring(n):
    return 8 <= n <= 16


def solution(mesh):
    in_specs = (
        P("dp", "mp"),
        P("dp", "mp"),
        P(),
        P("dp", None, "mp"),
        P("mp", "dp"),
        P(),
        P("dp", "mp"),
        P("mp", "dp"),
        P(),
        P("dp", None, "mp"),
        P("mp", "dp"),
        P(),
        P("dp", "mp"),
        P("mp", "dp"),
    )
    out_specs = (P("dp", "mp"), P("dp", "mp"))
    sizes = (mesh.shape["dp"], mesh.shape["mp"])

    def body(*args):
        return local(sizes, *args)

    return jax.shard_map(body, mesh=mesh, in_specs=in_specs, out_specs=out_specs, check_vma=False)
```

profile of v0, /device:TPU:0, one launch (start us, length us, event | category | flops | bytes accessed | tf_op | source)
XLA Modules:
  0.0 207.4 jit_solution(8668095175415523493)
XLA Ops:
  3.6 3.0 %collective-permute-start.34 = (bf16[72,2304]{1,0:T(8,128)(2,1)S(1)}, bf16[72,2304]{1,0:T(8,128)(2,1)}, u32[]{:S(2)}, u32[]{:S(2)}) collective-permute-start(bf16[72,2304]{1,0:T(8,128)(2,1)S(1)} %concatenate.14.rest_0_), channel_id=1, source_target_pairs={{0,4},{4,12},{8,0},{12,20},{16,8},{20,28},{24,16},{28,24},{2,10},{... | collective-permute-start | bytes 995336 | tf_op jit(solution)/shard_map/ppermute | solution.py:417
  6.7 1.6 collective-permute-start.2
  9.9 4.7 %collective-permute-done.2.rest_2_ = bf16[64,2048]{1,0:T(8,128)(2,1)S(1)} collective-permute-done((bf16[64,2048]{1,0:T(8,128)(2,1)S(1)}, bf16[64,2048]{1,0:T(8,128)(2,1)S(1)}, u32[]{:S(2)}, u32[]{:S(2)}) %collective-permute-start.2) | collective-permute-done | bytes 262176 | tf_op jit(solution)/shard_map/ppermute | solution.py:417
  14.6 1.9 collective-permute-start.32
  16.5 1.5 collective-permute-start.18
  18.1 1.6 collective-permute-start.4
  20.9 7.7 %collective-permute-done.4.rest_4_ = bf16[64,2048]{1,0:T(8,128)(2,1)} collective-permute-done((bf16[64,2048]{1,0:T(8,128)(2,1)S(1)}, bf16[64,2048]{1,0:T(8,128)(2,1)}, u32[]{:S(2)}, u32[]{:S(2)}) %collective-permute-start.4) | collective-permute-done | bytes 262176 | tf_op jit(solution)/shard_map/ppermute | solution.py:417
  28.6 1.5 collective-permute-start.50
  32.2 1.6 collective-permute-start.36
  34.5 1.6 collective-permute-start.6
  36.0 6.5 %collective-permute-done.36.rest_4_ = bf16[72,2304]{1,0:T(8,128)(2,1)} collective-permute-done((bf16[72,2304]{1,0:T(8,128)(2,1)}, bf16[72,2304]{1,0:T(8,128)(2,1)}, u32[]{:S(2)}, u32[]{:S(2)}) %collective-permute-start.36) | collective-permute-done | bytes 331808 | tf_op jit(solution)/shard_map/ppermute | solution.py:417
  46.8 1.6 collective-permute-start.20
  49.9 1.5 collective-permute-start.52
  52.7 1.5 collective-permute-done.7.rest_7_
  54.3 1.5 collective-permute-start.10
  55.8 2.6 %collective-permute-done.20.refs_4_ = bf16[128,2048]{1,0:T(8,128)(2,1)S(1)} collective-permute-done((bf16[128,2048]{1,0:T(8,128)(2,1)}, bf16[128,2048]{1,0:T(8,128)(2,1)S(1)}, u32[]{:S(2)}, u32[]{:S(2)}) %collective-permute-start.20) | collective-permute-done | bytes 524320 | tf_op jit(solution)/shard_map/ppermute | solution.py:417
  59.9 5.2 %collective-permute-done.52.refs_4_ = bf16[144,2176]{1,0:T(8,128)(2,1)S(1)} collective-permute-done((bf16[144,2176]{1,0:T(8,128)(2,1)S(1)}, bf16[144,2176]{1,0:T(8,128)(2,1)S(1)}, u32[]{:S(2)}, u32[]{:S(2)}) %collective-permute-start.52) | collective-permute-done | bytes 626720 | tf_op jit(solution)/shard_map/ppermute | solution.py:417
  67.9 1.5 collective-permute-start.54
  69.4 7.6 %collective-permute-done.40.rest_8_ = bf16[72,2304]{1,0:T(8,128)(2,1)S(1)} collective-permute-done((bf16[72,2304]{1,0:T(8,128)(2,1)S(1)}, bf16[72,2304]{1,0:T(8,128)(2,1)S(1)}, u32[]{:S(2)}, u32[]{:S(2)}) %collective-permute-start.40) | collective-permute-done | bytes 331808 | tf_op jit(solution)/shard_map/ppermute | solution.py:417
  78.6 1.6 collective-permute-start.42
  80.6 5.9 %collective-permute-done.12.rest_12_ = bf16[64,2048]{1,0:T(8,128)(2,1)S(1)} collective-permute-done((bf16[64,2048]{1,0:T(8,128)(2,1)S(1)}, bf16[64,2048]{1,0:T(8,128)(2,1)S(1)}, u32[]{:S(2)}, u32[]{:S(2)}) %collective-permute-start.12) | collective-permute-done | bytes 262176 | tf_op jit(solution)/shard_map/ppermute | solution.py:417
  86.6 1.5 collective-permute-start.24
  88.1 2.0 collective-permute-done.42.rest_10_
  91.6 1.6 collective-permute-start.56
  93.2 5.3 %collective-permute-done.14.rest_14_ = bf16[64,2048]{1,0:T(8,128)(2,1)S(1)} collective-permute-done((bf16[64,2048]{1,0:T(8,128)(2,1)S(1)}, bf16[64,2048]{1,0:T(8,128)(2,1)S(1)}, u32[]{:S(2)}, u32[]{:S(2)}) %collective-permute-start.14) | collective-permute-done | bytes 262176 | tf_op jit(solution)/shard_map/ppermute | solution.py:417
  100.1 1.6 collective-permute-start.26
  101.7 7.1 %collective-permute-done.44.rest_12_ = bf16[72,2304]{1,0:T(8,128)(2,1)S(1)} collective-permute-done((bf16[72,2304]{1,0:T(8,128)(2,1)S(1)}, bf16[72,2304]{1,0:T(8,128)(2,1)S(1)}, u32[]{:S(2)}, u32[]{:S(2)}) %collective-permute-start.44) | collective-permute-done | bytes 331808 | tf_op jit(solution)/shard_map/ppermute | solution.py:417
  108.8 1.5 collective-permute-start.58
  110.4 1.6 collective-permute-start.46
  115.8 3.6 %shard_map.158 = (bf16[1024,2048]{1,0:T(8,128)(2,1)S(1)}, bf16[512,1024]{1,0:T(8,128)(2,1)S(1)}, bf16[512,1536]{1,0:T(8,128)(2,1)S(1)}) custom-call(s32[16]{0:T(128)S(1)} %dynamic-slice_bitcast_fusion.table, bf16[512,512]{1,0:T(8,128)(2,1)S(1)} %copy-done.6, bf16[512,512]{1,0:T(8,128)(2,1)S(1)} %copy-done.8, f32[1,1024]{1,0:T(1,128)S(1)} %bitcast.23, ...), custom_call_target="tpu_custom_call" | custom-call | tf_op jit(solution)/shard_map/pallas_call | solution.py:173
  119.5 3.0 %shard_map.159 = (f32[512,1024]{1,0:T(8,128)S(1)}, bf16[512,1024]{1,0:T(8,128)(2,1)S(1)}) custom-call(bf16[1024,2048]{1,0:T(8,128)(2,1)S(1)} %get-tuple-element.30.weight, bf16[512,1024]{1,0:T(8,128)(2,1)S(1)} %get-tuple-element.31.whole, bf16[512,1536]{1,0:T(8,128)(2,1)S(1)} %get-tuple-element.32.projected), custom_call_target="tpu_custom_call" | custom-call | tf_op jit(solution)/shard_map/pallas_call | solution.py:198
  123.2 1.6 collective-permute-start.28
  125.3 1.6 collective-permute-start.60
  127.4 4.9 %collective-permute-done.28.refs_12_ = bf16[128,2048]{1,0:T(8,128)(2,1)S(1)} collective-permute-done((bf16[128,2048]{1,0:T(8,128)(2,1)S(1)}, bf16[128,2048]{1,0:T(8,128)(2,1)S(1)}, u32[]{:S(2)}, u32[]{:S(2)}) %collective-permute-start.28) | collective-permute-done | bytes 524320 | tf_op jit(solution)/shard_map/ppermute | solution.py:417
  132.3 1.6 collective-permute-start.30
  133.9 7.6 %shard_map.163 = (bf16[1152,2304]{1,0:T(8,128)(2,1)S(1)}, bf16[512,1152]{1,0:T(8,128)(2,1)S(1)}, bf16[512,1792]{1,0:T(8,128)(2,1)S(1)}) custom-call(s32[16]{0:T(128)S(1)} %dynamic-slice_bitcast_fusion.table, bf16[576,512]{1,0:T(8,128)(2,1)} %bitcast.8.own_ref, bf16[576,512]{1,0:T(8,128)(2,1)} %collective-permute-done.32.other_ref, ...), custom_call_target="tpu_custom_call" | custom-call | tf_op jit(solution)/shard_map/pallas_call | solution.py:173
  141.5 3.8 %shard_map.164 = (f32[512,1152]{1,0:T(8,128)S(1)}, bf16[512,1152]{1,0:T(8,128)(2,1)S(1)}) custom-call(bf16[1152,2304]{1,0:T(8,128)(2,1)S(1)} %get-tuple-element.41.weight, bf16[512,1152]{1,0:T(8,128)(2,1)S(1)} %get-tuple-element.42.whole, bf16[512,1792]{1,0:T(8,128)(2,1)S(1)} %get-tuple-element.43.projected), custom_call_target="tpu_custom_call" | custom-call | tf_op jit(solution)/shard_map/pallas_call | solution.py:198
  145.3 1.6 collective-permute-start.48
  146.9 1.6 collective-permute-start.62
  152.0 5.3 %collective-permute-done.62.refs_2_ = bf16[144,2176]{1,0:T(8,128)(2,1)} collective-permute-done((bf16[144,2176]{1,0:T(8,128)(2,1)S(1)}, bf16[144,2176]{1,0:T(8,128)(2,1)}, u32[]{:S(2)}, u32[]{:S(2)}) %collective-permute-start.62) | collective-permute-done | bytes 626720 | tf_op jit(solution)/shard_map/ppermute | solution.py:417
  158.1 2.4 %shard_map.161 = (bf16[16,64,2048]{2,1,0:T(8,128)(2,1)S(1)}, bf16[16,64,2048]{2,1,0:T(8,128)(2,1)S(1)}) custom-call(s32[16]{0:T(128)S(1)} %dynamic-slice_bitcast_fusion.table, bf16[128,2048]{1,0:T(8,128)(2,1)S(1)} %pad_maximum_fusion.refs_0_, bf16[128,2048]{1,0:T(8,128)(2,1)} %collective-permute-done.17.refs_1_, ...), custom_call_target="tpu_custom_call" | custom-call | tf_op jit(solution)/shard_map/pallas_call | solution.py:330
  160.5 5.4 %shard_map.162 = (bf16[512,512]{1,0:T(8,128)(2,1)}, bf16[512,2048]{1,0:T(8,128)(2,1)S(1)}, bf16[16,64,2048]{2,1,0:T(8,128)(2,1)S(1)}, bf16[16,64,2048]{2,1,0:T(8,128)(2,1)S(1)}) custom-call(s32[16]{0:T(128)S(1)} %dynamic-slice_bitcast_fusion.table, bf16[512,1024]{1,0:T(8,128)(2,1)S(1)} %get-tuple-element.35.tokens_ref, ...), custom_call_target="tpu_custom_call", output_to_operand_aliasing={{2}: (2, {}), {3}: (3, {})} | custom-call | tf_op jit(solution)/shard_map/pallas_call | solution.py:351
  166.0 7.5 %collective-permute-done.48.got_ref = bf16[512,1152]{1,0:T(8,128)(2,1)S(1)} collective-permute-done((bf16[512,1152]{1,0:T(8,128)(2,1)S(1)}, bf16[512,1152]{1,0:T(8,128)(2,1)S(1)}, u32[]{:S(2)}, u32[]{:S(2)}) %collective-permute-start.48) | collective-permute-done | bytes 1179680 | tf_op jit(solution)/shard_map/ppermute | solution.py:389
  181.0 3.5 %shard_map.166 = (bf16[16,72,2176]{2,1,0:T(8,128)(2,1)S(1)}, bf16[16,72,2176]{2,1,0:T(8,128)(2,1)S(1)}) custom-call(s32[16]{0:T(128)S(1)} %dynamic-slice_bitcast_fusion.table, bf16[144,2176]{1,0:T(8,128)(2,1)S(1)} %fusion.2.refs_0_, bf16[144,2176]{1,0:T(8,128)(2,1)S(1)} %collective-permute-done.49.refs_1_, ...), custom_call_target="tpu_custom_call" | custom-call | tf_op jit(solution)/shard_map/pallas_call | solution.py:330
  184.5 7.6 %shard_map.167 = (bf16[576,512]{1,0:T(8,128)(2,1)}, bf16[512,2176]{1,0:T(8,128)(2,1)S(1)}, bf16[16,72,2176]{2,1,0:T(8,128)(2,1)S(1)}, bf16[16,72,2176]{2,1,0:T(8,128)(2,1)S(1)}) custom-call(s32[16]{0:T(128)S(1)} %dynamic-slice_bitcast_fusion.table, bf16[512,1152]{1,0:T(8,128)(2,1)S(1)} %get-tuple-element.46.tokens_ref, ...), custom_call_target="tpu_custom_call", output_to_operand_aliasing={{2}: (2, {}), {3}: (3, {})} | custom-call | tf_op jit(solution)/shard_map/pallas_call | solution.py:351
  192.1 1.6 collective-permute-start.65
  193.6 2.7 %finish.1 = (f32[512,512]{1,0:T(8,128)S(1)}, f32[576,512]{1,0:T(8,128)S(1)}) custom-call(bf16[512,2048]{1,0:T(8,128)(2,1)S(1)} %get-tuple-element.38.refs_0_, bf16[512,512]{1,0:T(8,128)(2,1)S(1)} %get-tuple-element.39.refs_1_, bf16[16,64,2048]{2,1,0:T(8,128)(2,1)S(1)} %get-tuple-element.40.refs_2_, bf16[512,2176]{1,0:T(8,128)(2,1)S(1)} %get-tuple-element.49.refs_3_, ...), custom_call_target="tpu_custom_call" | custom-call | tf_op jit(solution)/shard_map/finish/pallas_call | solution.py:378
  197.3 9.1 %collective-permute-done.65 = bf16[576,512]{1,0:T(8,128)(2,1)S(1)} collective-permute-done((bf16[576,512]{1,0:T(8,128)(2,1)}, bf16[576,512]{1,0:T(8,128)(2,1)S(1)}, u32[]{:S(2)}, u32[]{:S(2)}) %collective-permute-start.65) | collective-permute-done | bytes 589856 | tf_op jit(solution)/shard_map/ppermute | solution.py:389
  (172 shorter events, 44.4 us)
Async XLA Ops:
  3.6 14.5 %collective-permute-start.34 = (bf16[72,2304]{1,0:T(8,128)(2,1)S(1)}, bf16[72,2304]{1,0:T(8,128)(2,1)}, u32[]{:S(2)}, u32[]{:S(2)}) collective-permute-start(bf16[72,2304]{1,0:T(8,128)(2,1)S(1)} %concatenate.14.rest_0_), channel_id=1, source_target_pairs={{0,4},{4,12},{8,0},{12,20},{16,8},{20,28},{24,16},{28,24},{2,10},{... | collective-permute-start | bytes 995336 | tf_op jit(solution)/shard_map/ppermute | solution.py:417
  6.6 13.0 %collective-permute-start.33 = (bf16[72,2304]{1,0:T(8,128)(2,1)S(1)}, bf16[72,2304]{1,0:T(8,128)(2,1)S(1)}, u32[]{:S(2)}, u32[]{:S(2)}) collective-permute-start(bf16[72,2304]{1,0:T(8,128)(2,1)S(1)} %concatenate.14.rest_0_), channel_id=1, source_target_pairs={{0,2},{2,0},{4,6},{6,4},{8,10},{10,8},{12,14},{14,12},{16,18},{18,... | collective-permute-start | bytes 995336 | tf_op jit(solution)/shard_map/ppermute | solution.py:414
  8.3 22.5 %collective-permute-start = (bf16[512,512]{1,0:T(8,128)(2,1)S(1)}, bf16[512,512]{1,0:T(8,128)(2,1)S(1)}, u32[]{:S(2)}, u32[]{:S(2)}) collective-permute-start(bf16[512,512]{1,0:T(8,128)(2,1)S(1)} %copy-done.6), channel_id=1, source_target_pairs={{0,1},{1,0},{2,3},{3,2},{4,5},{5,4},{6,7},{7,6},{8,9},{9,8},{10,11... | collective-permute-start | bytes 1572872 | tf_op jit(solution)/shard_map/ppermute | solution.py:389
  14.6 21.4 %collective-permute-start.32 = (bf16[576,512]{1,0:T(8,128)(2,1)}, bf16[576,512]{1,0:T(8,128)(2,1)}, u32[]{:S(2)}, u32[]{:S(2)}) collective-permute-start(bf16[576,512]{1,0:T(8,128)(2,1)} %bitcast.8.own_ref), channel_id=1, source_target_pairs={{0,1},{1,0},{2,3},{3,2},{4,5},{5,4},{6,7},{7,6},{8,9},{9,8},{10,11... | collective-permute-start | bytes 1769480 | tf_op jit(solution)/shard_map/ppermute | solution.py:389
  16.5 15.6 %collective-permute-start.18 = (bf16[128,2048]{1,0:T(8,128)(2,1)S(1)}, bf16[128,2048]{1,0:T(8,128)(2,1)}, u32[]{:S(2)}, u32[]{:S(2)}) collective-permute-start(bf16[128,2048]{1,0:T(8,128)(2,1)S(1)} %pad_maximum_fusion.refs_0_), channel_id=1, source_target_pairs={{0,4},{4,12},{8,0},{12,20},{16,8},{20,28},{24,16},{28,24},{2,10},{... | collective-permute-start | bytes 1572872 | tf_op jit(solution)/shard_map/ppermute | solution.py:417
  18.1 10.6 %collective-permute-start.4 = (bf16[64,2048]{1,0:T(8,128)(2,1)S(1)}, bf16[64,2048]{1,0:T(8,128)(2,1)}, u32[]{:S(2)}, u32[]{:S(2)}) collective-permute-start(bf16[64,2048]{1,0:T(8,128)(2,1)S(1)} %collective-permute-done.2.rest_2_), channel_id=1, source_target_pairs={{0,4},{4,12},{8,0},{12,20},{16,8},{20,28},{24,16},{28,24},{2,10},{... | collective-permute-start | bytes 786440 | tf_op jit(solution)/shard_map/ppermute | solution.py:417
  19.6 10.5 %collective-permute-start.3 = (bf16[64,2048]{1,0:T(8,128)(2,1)S(1)}, bf16[64,2048]{1,0:T(8,128)(2,1)S(1)}, u32[]{:S(2)}, u32[]{:S(2)}) collective-permute-start(bf16[64,2048]{1,0:T(8,128)(2,1)S(1)} %collective-permute-done.2.rest_2_), channel_id=1, source_target_pairs={{0,2},{2,0},{4,6},{6,4},{8,10},{10,8},{12,14},{14,12},{16,18},{18,... | collective-permute-start | bytes 786440 | tf_op jit(solution)/shard_map/ppermute | solution.py:414
  28.6 15.5 %collective-permute-start.50 = (bf16[144,2176]{1,0:T(8,128)(2,1)S(1)}, bf16[144,2176]{1,0:T(8,128)(2,1)S(1)}, u32[]{:S(2)}, u32[]{:S(2)}) collective-permute-start(bf16[144,2176]{1,0:T(8,128)(2,1)S(1)} %fusion.2.refs_0_), channel_id=1, source_target_pairs={{0,4},{4,12},{8,0},{12,20},{16,8},{20,28},{24,16},{28,24},{2,10},{... | collective-permute-start | bytes 1880072 | tf_op jit(solution)/shard_map/ppermute | solution.py:417
  30.9 13.2 %collective-permute-start.49 = (bf16[144,2176]{1,0:T(8,128)(2,1)S(1)}, bf16[144,2176]{1,0:T(8,128)(2,1)S(1)}, u32[]{:S(2)}, u32[]{:S(2)}) collective-permute-start(bf16[144,2176]{1,0:T(8,128)(2,1)S(1)} %fusion.2.refs_0_), channel_id=1, source_target_pairs={{0,2},{2,0},{4,6},{6,4},{8,10},{10,8},{12,14},{14,12},{16,18},{18,... | collective-permute-start | bytes 1880072 | tf_op jit(solution)/shard_map/ppermute | solution.py:414
  32.2 10.4 %collective-permute-start.36 = (bf16[72,2304]{1,0:T(8,128)(2,1)}, bf16[72,2304]{1,0:T(8,128)(2,1)}, u32[]{:S(2)}, u32[]{:S(2)}) collective-permute-start(bf16[72,2304]{1,0:T(8,128)(2,1)} %collective-permute-done.34.rest_2_), channel_id=1, source_target_pairs={{0,4},{4,12},{8,0},{12,20},{16,8},{20,28},{24,16},{28,24},{2,10},{... | collective-permute-start | bytes 995336 | tf_op jit(solution)/shard_map/ppermute | solution.py:417
  34.5 10.8 %collective-permute-start.6 = (bf16[64,2048]{1,0:T(8,128)(2,1)}, bf16[64,2048]{1,0:T(8,128)(2,1)S(1)}, u32[]{:S(2)}, u32[]{:S(2)}) collective-permute-start(bf16[64,2048]{1,0:T(8,128)(2,1)} %collective-permute-done.4.rest_4_), channel_id=1, source_target_pairs={{0,4},{4,12},{8,0},{12,20},{16,8},{20,28},{24,16},{28,24},{2,10},{... | collective-permute-start | bytes 786440 | tf_op jit(solution)/shard_map/ppermute | solution.py:417
  36.0 10.8 %collective-permute-start.35 = (bf16[72,2304]{1,0:T(8,128)(2,1)}, bf16[72,2304]{1,0:T(8,128)(2,1)S(1)}, u32[]{:S(2)}, u32[]{:S(2)}) collective-permute-start(bf16[72,2304]{1,0:T(8,128)(2,1)} %collective-permute-done.34.rest_2_), channel_id=1, source_target_pairs={{0,2},{2,0},{4,6},{6,4},{8,10},{10,8},{12,14},{14,12},{16,18},{18,... | collective-permute-start | bytes 995336 | tf_op jit(solution)/shard_map/ppermute | solution.py:414
  46.8 11.5 %collective-permute-start.20 = (bf16[128,2048]{1,0:T(8,128)(2,1)}, bf16[128,2048]{1,0:T(8,128)(2,1)S(1)}, u32[]{:S(2)}, u32[]{:S(2)}) collective-permute-start(bf16[128,2048]{1,0:T(8,128)(2,1)} %collective-permute-done.18.refs_2_), channel_id=1, source_target_pairs={{0,4},{4,12},{8,0},{12,20},{16,8},{20,28},{24,16},{28,24},{2,10},{... | collective-permute-start | bytes 1572872 | tf_op jit(solution)/shard_map/ppermute | solution.py:417
  48.4 11.5 %collective-permute-start.19 = (bf16[128,2048]{1,0:T(8,128)(2,1)}, bf16[128,2048]{1,0:T(8,128)(2,1)S(1)}, u32[]{:S(2)}, u32[]{:S(2)}) collective-permute-start(bf16[128,2048]{1,0:T(8,128)(2,1)} %collective-permute-done.18.refs_2_), channel_id=1, source_target_pairs={{0,2},{2,0},{4,6},{6,4},{8,10},{10,8},{12,14},{14,12},{16,18},{18,... | collective-permute-start | bytes 1572872 | tf_op jit(solution)/shard_map/ppermute | solution.py:414
  49.9 15.1 %collective-permute-start.52 = (bf16[144,2176]{1,0:T(8,128)(2,1)S(1)}, bf16[144,2176]{1,0:T(8,128)(2,1)S(1)}, u32[]{:S(2)}, u32[]{:S(2)}) collective-permute-start(bf16[144,2176]{1,0:T(8,128)(2,1)S(1)} %collective-permute-done.50.refs_2_), channel_id=1, source_target_pairs={{0,4},{4,12},{8,0},{12,20},{16,8},{20,28},{24,16},{28,24},{2,10},{... | collective-permute-start | bytes 1880072 | tf_op jit(solution)/shard_map/ppermute | solution.py:417
  51.4 15.1 %collective-permute-start.51 = (bf16[144,2176]{1,0:T(8,128)(2,1)S(1)}, bf16[144,2176]{1,0:T(8,128)(2,1)S(1)}, u32[]{:S(2)}, u32[]{:S(2)}) collective-permute-start(bf16[144,2176]{1,0:T(8,128)(2,1)S(1)} %collective-permute-done.50.refs_2_), channel_id=1, source_target_pairs={{0,2},{2,0},{4,6},{6,4},{8,10},{10,8},{12,14},{14,12},{16,18},{18,... | collective-permute-start | bytes 1880072 | tf_op jit(solution)/shard_map/ppermute | solution.py:414
  54.3 13.6 %collective-permute-start.10 = (bf16[64,2048]{1,0:T(8,128)(2,1)S(1)}, bf16[64,2048]{1,0:T(8,128)(2,1)S(1)}, u32[]{:S(2)}, u32[]{:S(2)}) collective-permute-start(bf16[64,2048]{1,0:T(8,128)(2,1)S(1)} %collective-permute-done.8.rest_8_), channel_id=1, source_target_pairs={{0,4},{4,12},{8,0},{12,20},{16,8},{20,28},{24,16},{28,24},{2,10},{... | collective-permute-start | bytes 786440 | tf_op jit(solution)/shard_map/ppermute | solution.py:417
  58.3 21.8 %collective-permute-start.22 = (bf16[128,2048]{1,0:T(8,128)(2,1)S(1)}, bf16[128,2048]{1,0:T(8,128)(2,1)S(1)}, u32[]{:S(2)}, u32[]{:S(2)}) collective-permute-start(bf16[128,2048]{1,0:T(8,128)(2,1)S(1)} %collective-permute-done.20.refs_4_), channel_id=1, source_target_pairs={{0,4},{4,12},{8,0},{12,20},{16,8},{20,28},{24,16},{28,24},{2,10},{... | collective-permute-start | bytes 1572872 | tf_op jit(solution)/shard_map/ppermute | solution.py:417
  65.0 12.0 %collective-permute-start.40 = (bf16[72,2304]{1,0:T(8,128)(2,1)S(1)}, bf16[72,2304]{1,0:T(8,128)(2,1)S(1)}, u32[]{:S(2)}, u32[]{:S(2)}) collective-permute-start(bf16[72,2304]{1,0:T(8,128)(2,1)S(1)} %collective-permute-done.38.rest_6_), channel_id=1, source_target_pairs={{0,4},{4,12},{8,0},{12,20},{16,8},{20,28},{24,16},{28,24},{2,10},{... | collective-permute-start | bytes 995336 | tf_op jit(solution)/shard_map/ppermute | solution.py:417
  66.6 12.0 %collective-permute-start.39 = (bf16[72,2304]{1,0:T(8,128)(2,1)S(1)}, bf16[72,2304]{1,0:T(8,128)(2,1)S(1)}, u32[]{:S(2)}, u32[]{:S(2)}) collective-permute-start(bf16[72,2304]{1,0:T(8,128)(2,1)S(1)} %collective-permute-done.38.rest_6_), channel_id=1, source_target_pairs={{0,2},{2,0},{4,6},{6,4},{8,10},{10,8},{12,14},{14,12},{16,18},{18,... | collective-permute-start | bytes 995336 | tf_op jit(solution)/shard_map/ppermute | solution.py:414
  67.9 12.3 %collective-permute-start.21 = (bf16[128,2048]{1,0:T(8,128)(2,1)S(1)}, bf16[128,2048]{1,0:T(8,128)(2,1)S(1)}, u32[]{:S(2)}, u32[]{:S(2)}) collective-permute-start(bf16[128,2048]{1,0:T(8,128)(2,1)S(1)} %collective-permute-done.20.refs_4_), channel_id=1, source_target_pairs={{0,2},{2,0},{4,6},{6,4},{8,10},{10,8},{12,14},{14,12},{16,18},{18,... | collective-permute-start | bytes 1572872 | tf_op jit(solution)/shard_map/ppermute | solution.py:414
  67.9 23.8 %collective-permute-start.54 = (bf16[144,2176]{1,0:T(8,128)(2,1)S(1)}, bf16[144,2176]{1,0:T(8,128)(2,1)S(1)}, u32[]{:S(2)}, u32[]{:S(2)}) collective-permute-start(bf16[144,2176]{1,0:T(8,128)(2,1)S(1)} %collective-permute-done.52.refs_4_), channel_id=1, source_target_pairs={{0,4},{4,12},{8,0},{12,20},{16,8},{20,28},{24,16},{28,24},{2,10},{... | collective-permute-start | bytes 1880072 | tf_op jit(solution)/shard_map/ppermute | solution.py:417
  77.0 9.5 %collective-permute-start.12 = (bf16[64,2048]{1,0:T(8,128)(2,1)S(1)}, bf16[64,2048]{1,0:T(8,128)(2,1)S(1)}, u32[]{:S(2)}, u32[]{:S(2)}) collective-permute-start(bf16[64,2048]{1,0:T(8,128)(2,1)S(1)} %collective-permute-done.10.rest_10_), channel_id=1, source_target_pairs={{0,4},{4,12},{8,0},{12,20},{16,8},{20,28},{24,16},{28,24},{2,10},{... | collective-permute-start | bytes 786440 | tf_op jit(solution)/shard_map/ppermute | solution.py:417
  78.6 11.6 %collective-permute-start.42 = (bf16[72,2304]{1,0:T(8,128)(2,1)S(1)}, bf16[72,2304]{1,0:T(8,128)(2,1)S(1)}, u32[]{:S(2)}, u32[]{:S(2)}) collective-permute-start(bf16[72,2304]{1,0:T(8,128)(2,1)S(1)} %collective-permute-done.40.rest_8_), channel_id=1, source_target_pairs={{0,4},{4,12},{8,0},{12,20},{16,8},{20,28},{24,16},{28,24},{2,10},{... | collective-permute-start | bytes 995336 | tf_op jit(solution)/shard_map/ppermute | solution.py:417
  80.1 13.1 %collective-permute-start.41 = (bf16[72,2304]{1,0:T(8,128)(2,1)S(1)}, bf16[72,2304]{1,0:T(8,128)(2,1)S(1)}, u32[]{:S(2)}, u32[]{:S(2)}) collective-permute-start(bf16[72,2304]{1,0:T(8,128)(2,1)S(1)} %collective-permute-done.40.rest_8_), channel_id=1, source_target_pairs={{0,2},{2,0},{4,6},{6,4},{8,10},{10,8},{12,14},{14,12},{16,18},{18,... | collective-permute-start | bytes 995336 | tf_op jit(solution)/shard_map/ppermute | solution.py:414
  86.6 15.2 %collective-permute-start.53 = (bf16[144,2176]{1,0:T(8,128)(2,1)S(1)}, bf16[144,2176]{1,0:T(8,128)(2,1)S(1)}, u32[]{:S(2)}, u32[]{:S(2)}) collective-permute-start(bf16[144,2176]{1,0:T(8,128)(2,1)S(1)} %collective-permute-done.52.refs_4_), channel_id=1, source_target_pairs={{0,2},{2,0},{4,6},{6,4},{8,10},{10,8},{12,14},{14,12},{16,18},{18,... | collective-permute-start | bytes 1880072 | tf_op jit(solution)/shard_map/ppermute | solution.py:414
  86.6 13.5 %collective-permute-start.24 = (bf16[128,2048]{1,0:T(8,128)(2,1)S(1)}, bf16[128,2048]{1,0:T(8,128)(2,1)S(1)}, u32[]{:S(2)}, u32[]{:S(2)}) collective-permute-start(bf16[128,2048]{1,0:T(8,128)(2,1)S(1)} %collective-permute-done.22.refs_6_), channel_id=1, source_target_pairs={{0,4},{4,12},{8,0},{12,20},{16,8},{20,28},{24,16},{28,24},{2,10},{... | collective-permute-start | bytes 1572872 | tf_op jit(solution)/shard_map/ppermute | solution.py:417
  91.6 17.2 %collective-permute-start.56 = (bf16[144,2176]{1,0:T(8,128)(2,1)S(1)}, bf16[144,2176]{1,0:T(8,128)(2,1)S(1)}, u32[]{:S(2)}, u32[]{:S(2)}) collective-permute-start(bf16[144,2176]{1,0:T(8,128)(2,1)S(1)} %collective-permute-done.54.refs_6_), channel_id=1, source_target_pairs={{0,4},{4,12},{8,0},{12,20},{16,8},{20,28},{24,16},{28,24},{2,10},{... | collective-permute-start | bytes 1880072 | tf_op jit(solution)/shard_map/ppermute | solution.py:417
  98.6 10.3 %collective-permute-start.44 = (bf16[72,2304]{1,0:T(8,128)(2,1)S(1)}, bf16[72,2304]{1,0:T(8,128)(2,1)S(1)}, u32[]{:S(2)}, u32[]{:S(2)}) collective-permute-start(bf16[72,2304]{1,0:T(8,128)(2,1)S(1)} %collective-permute-done.42.rest_10_), channel_id=1, source_target_pairs={{0,4},{4,12},{8,0},{12,20},{16,8},{20,28},{24,16},{28,24},{2,10},{... | collective-permute-start | bytes 995336 | tf_op jit(solution)/shard_map/ppermute | solution.py:417
  100.1 22.5 %collective-permute-start.23 = (bf16[128,2048]{1,0:T(8,128)(2,1)S(1)}, bf16[128,2048]{1,0:T(8,128)(2,1)S(1)}, u32[]{:S(2)}, u32[]{:S(2)}) collective-permute-start(bf16[128,2048]{1,0:T(8,128)(2,1)S(1)} %collective-permute-done.22.refs_6_), channel_id=1, source_target_pairs={{0,2},{2,0},{4,6},{6,4},{8,10},{10,8},{12,14},{14,12},{16,18},{18,... | collective-permute-start | bytes 1572872 | tf_op jit(solution)/shard_map/ppermute | solution.py:414
  100.1 23.1 %collective-permute-start.26 = (bf16[128,2048]{1,0:T(8,128)(2,1)S(1)}, bf16[128,2048]{1,0:T(8,128)(2,1)S(1)}, u32[]{:S(2)}, u32[]{:S(2)}) collective-permute-start(bf16[128,2048]{1,0:T(8,128)(2,1)S(1)} %collective-permute-done.24.refs_8_), channel_id=1, source_target_pairs={{0,4},{4,12},{8,0},{12,20},{16,8},{20,28},{24,16},{28,24},{2,10},{... | collective-permute-start | bytes 1572872 | tf_op jit(solution)/shard_map/ppermute | solution.py:417
  108.8 16.4 %collective-permute-start.58 = (bf16[144,2176]{1,0:T(8,128)(2,1)S(1)}, bf16[144,2176]{1,0:T(8,128)(2,1)S(1)}, u32[]{:S(2)}, u32[]{:S(2)}) collective-permute-start(bf16[144,2176]{1,0:T(8,128)(2,1)S(1)} %collective-permute-done.56.refs_8_), channel_id=1, source_target_pairs={{0,4},{4,12},{8,0},{12,20},{16,8},{20,28},{24,16},{28,24},{2,10},{... | collective-permute-start | bytes 1880072 | tf_op jit(solution)/shard_map/ppermute | solution.py:417
  110.4 14.4 %collective-permute-start.46 = (bf16[72,2304]{1,0:T(8,128)(2,1)S(1)}, bf16[72,2304]{1,0:T(8,128)(2,1)S(1)}, u32[]{:S(2)}, u32[]{:S(2)}) collective-permute-start(bf16[72,2304]{1,0:T(8,128)(2,1)S(1)} %collective-permute-done.44.rest_12_), channel_id=1, source_target_pairs={{0,4},{4,12},{8,0},{12,20},{16,8},{20,28},{24,16},{28,24},{2,10},{... | collective-permute-start | bytes 995336 | tf_op jit(solution)/shard_map/ppermute | solution.py:417
  111.9 12.8 %collective-permute-start.45 = (bf16[72,2304]{1,0:T(8,128)(2,1)S(1)}, bf16[72,2304]{1,0:T(8,128)(2,1)S(1)}, u32[]{:S(2)}, u32[]{:S(2)}) collective-permute-start(bf16[72,2304]{1,0:T(8,128)(2,1)S(1)} %collective-permute-done.44.rest_12_), channel_id=1, source_target_pairs={{0,2},{2,0},{4,6},{6,4},{8,10},{10,8},{12,14},{14,12},{16,18},{18,... | collective-permute-start | bytes 995336 | tf_op jit(solution)/shard_map/ppermute | solution.py:414
  122.6 26.1 %collective-permute-start.16 = (bf16[512,1024]{1,0:T(8,128)(2,1)S(1)}, bf16[512,1024]{1,0:T(8,128)(2,1)S(1)}, u32[]{:S(2)}, u32[]{:S(2)}) collective-permute-start(bf16[512,1024]{1,0:T(8,128)(2,1)S(1)} %get-tuple-element.34), channel_id=1, source_target_pairs={{0,1},{1,0},{2,3},{3,2},{4,5},{5,4},{6,7},{7,6},{8,9},{9,8},{10,11... | collective-permute-start | bytes 3145736 | tf_op jit(solution)/shard_map/ppermute | solution.py:389
  123.2 9.2 %collective-permute-start.28 = (bf16[128,2048]{1,0:T(8,128)(2,1)S(1)}, bf16[128,2048]{1,0:T(8,128)(2,1)S(1)}, u32[]{:S(2)}, u32[]{:S(2)}) collective-permute-start(bf16[128,2048]{1,0:T(8,128)(2,1)S(1)} %collective-permute-done.26.refs_10_), channel_id=1, source_target_pairs={{0,4},{4,12},{8,0},{12,20},{16,8},{20,28},{24,16},{28,24},{2,10},{... | collective-permute-start | bytes 1572872 | tf_op jit(solution)/shard_map/ppermute | solution.py:417
  124.7 20.6 %collective-permute-start.55 = (bf16[144,2176]{1,0:T(8,128)(2,1)S(1)}, bf16[144,2176]{1,0:T(8,128)(2,1)S(1)}, u32[]{:S(2)}, u32[]{:S(2)}) collective-permute-start(bf16[144,2176]{1,0:T(8,128)(2,1)S(1)} %collective-permute-done.54.refs_6_), channel_id=1, source_target_pairs={{0,2},{2,0},{4,6},{6,4},{8,10},{10,8},{12,14},{14,12},{16,18},{18,... | collective-permute-start | bytes 1880072 | tf_op jit(solution)/shard_map/ppermute | solution.py:414
  125.3 21.6 %collective-permute-start.60 = (bf16[144,2176]{1,0:T(8,128)(2,1)S(1)}, bf16[144,2176]{1,0:T(8,128)(2,1)S(1)}, u32[]{:S(2)}, u32[]{:S(2)}) collective-permute-start(bf16[144,2176]{1,0:T(8,128)(2,1)S(1)} %collective-permute-done.58.refs_10_), channel_id=1, source_target_pairs={{0,4},{4,12},{8,0},{12,20},{16,8},{20,28},{24,16},{28,24},{2,10},{... | collective-permute-start | bytes 1880072 | tf_op jit(solution)/shard_map/ppermute | solution.py:417
  127.3 21.2 %collective-permute-start.25 = (bf16[128,2048]{1,0:T(8,128)(2,1)S(1)}, bf16[128,2048]{1,0:T(8,128)(2,1)S(1)}, u32[]{:S(2)}, u32[]{:S(2)}) collective-permute-start(bf16[128,2048]{1,0:T(8,128)(2,1)S(1)} %collective-permute-done.24.refs_8_), channel_id=1, source_target_pairs={{0,2},{2,0},{4,6},{6,4},{8,10},{10,8},{12,14},{14,12},{16,18},{18,... | collective-permute-start | bytes 1572872 | tf_op jit(solution)/shard_map/ppermute | solution.py:414
  132.3 16.6 %collective-permute-start.30 = (bf16[128,2048]{1,0:T(8,128)(2,1)S(1)}, bf16[128,2048]{1,0:T(8,128)(2,1)S(1)}, u32[]{:S(2)}, u32[]{:S(2)}) collective-permute-start(bf16[128,2048]{1,0:T(8,128)(2,1)S(1)} %collective-permute-done.28.refs_12_), channel_id=1, source_target_pairs={{0,4},{4,12},{8,0},{12,20},{16,8},{20,28},{24,16},{28,24},{2,10},{... | collective-permute-start | bytes 1572872 | tf_op jit(solution)/shard_map/ppermute | solution.py:417
  145.3 28.1 %collective-permute-start.48 = (bf16[512,1152]{1,0:T(8,128)(2,1)S(1)}, bf16[512,1152]{1,0:T(8,128)(2,1)S(1)}, u32[]{:S(2)}, u32[]{:S(2)}) collective-permute-start(bf16[512,1152]{1,0:T(8,128)(2,1)S(1)} %get-tuple-element.45), channel_id=1, source_target_pairs={{0,1},{1,0},{2,3},{3,2},{4,5},{5,4},{6,7},{7,6},{8,9},{9,8},{10,11... | collective-permute-start | bytes 3538952 | tf_op jit(solution)/shard_map/ppermute | solution.py:389
  146.9 10.4 %collective-permute-start.62 = (bf16[144,2176]{1,0:T(8,128)(2,1)S(1)}, bf16[144,2176]{1,0:T(8,128)(2,1)}, u32[]{:S(2)}, u32[]{:S(2)}) collective-permute-start(bf16[144,2176]{1,0:T(8,128)(2,1)S(1)} %collective-permute-done.60.refs_12_), channel_id=1, source_target_pairs={{0,4},{4,12},{8,0},{12,20},{16,8},{20,28},{24,16},{28,24},{2,10},{... | collective-permute-start | bytes 1880072 | tf_op jit(solution)/shard_map/ppermute | solution.py:417
  150.4 24.9 %collective-permute-start.57 = (bf16[144,2176]{1,0:T(8,128)(2,1)S(1)}, bf16[144,2176]{1,0:T(8,128)(2,1)S(1)}, u32[]{:S(2)}, u32[]{:S(2)}) collective-permute-start(bf16[144,2176]{1,0:T(8,128)(2,1)S(1)} %collective-permute-done.56.refs_8_), channel_id=1, source_target_pairs={{0,2},{2,0},{4,6},{6,4},{8,10},{10,8},{12,14},{14,12},{16,18},{18,... | collective-permute-start | bytes 1880072 | tf_op jit(solution)/shard_map/ppermute | solution.py:414
  151.1 25.0 %collective-permute-start.59 = (bf16[144,2176]{1,0:T(8,128)(2,1)S(1)}, bf16[144,2176]{1,0:T(8,128)(2,1)S(1)}, u32[]{:S(2)}, u32[]{:S(2)}) collective-permute-start(bf16[144,2176]{1,0:T(8,128)(2,1)S(1)} %collective-permute-done.58.refs_10_), channel_id=1, source_target_pairs={{0,2},{2,0},{4,6},{6,4},{8,10},{10,8},{12,14},{14,12},{16,18},{18,... | collective-permute-start | bytes 1880072 | tf_op jit(solution)/shard_map/ppermute | solution.py:414
  151.9 25.1 %collective-permute-start.61 = (bf16[144,2176]{1,0:T(8,128)(2,1)S(1)}, bf16[144,2176]{1,0:T(8,128)(2,1)S(1)}, u32[]{:S(2)}, u32[]{:S(2)}) collective-permute-start(bf16[144,2176]{1,0:T(8,128)(2,1)S(1)} %collective-permute-done.60.refs_12_), channel_id=1, source_target_pairs={{0,2},{2,0},{4,6},{6,4},{8,10},{10,8},{12,14},{14,12},{16,18},{18,... | collective-permute-start | bytes 1880072 | tf_op jit(solution)/shard_map/ppermute | solution.py:414
  157.3 27.2 %collective-permute-start.63 = (bf16[144,2176]{1,0:T(8,128)(2,1)}, bf16[144,2176]{1,0:T(8,128)(2,1)}, u32[]{:S(2)}, u32[]{:S(2)}) collective-permute-start(bf16[144,2176]{1,0:T(8,128)(2,1)} %collective-permute-done.62.refs_2_), channel_id=1, source_target_pairs={{0,2},{2,0},{4,6},{6,4},{8,10},{10,8},{12,14},{14,12},{16,18},{18,... | collective-permute-start | bytes 1880072 | tf_op jit(solution)/shard_map/ppermute | solution.py:414
  173.5 22.8 %collective-permute-start.64 = (bf16[512,512]{1,0:T(8,128)(2,1)}, bf16[512,512]{1,0:T(8,128)(2,1)S(1)}, u32[]{:S(2)}, u32[]{:S(2)}) collective-permute-start(bf16[512,512]{1,0:T(8,128)(2,1)} %get-tuple-element.53), channel_id=1, source_target_pairs={{0,1},{1,0},{2,3},{3,2},{4,5},{5,4},{6,7},{7,6},{8,9},{9,8},{10,11... | collective-permute-start | bytes 1572872 | tf_op jit(solution)/shard_map/ppermute | solution.py:389
  192.1 14.3 %collective-permute-start.65 = (bf16[576,512]{1,0:T(8,128)(2,1)}, bf16[576,512]{1,0:T(8,128)(2,1)S(1)}, u32[]{:S(2)}, u32[]{:S(2)}) collective-permute-start(bf16[576,512]{1,0:T(8,128)(2,1)} %get-tuple-element.55), channel_id=1, source_target_pairs={{0,1},{1,0},{2,3},{3,2},{4,5},{5,4},{6,7},{7,6},{8,9},{9,8},{10,11... | collective-permute-start | bytes 1769480 | tf_op jit(solution)/shard_map/ppermute | solution.py:389
  (47 other events, 373.1 us)
where the time goes:
time: 208 us; the launch traced here: 207 us
  waiting for transfers between devices  90.2 us (43%)
  starting transfers between devices  55.7 us (27%)
  Pallas kernels  41.6 us (20%)
  local copies, waits for them, and re-layouts  15.5 us (7%)
  other arithmetic  3.29 us (2%)
    ppermute x28, waiting for transfers between devices, step(): return lax.ppermute(x, 'dp', self.hop)  69.7 us
    ppermute x28, starting transfers between devices, step(): return lax.ppermute(x, 'dp', self.hop)  44.9 us
    ppermute x6, waiting for transfers between devices, swap_mp(): return lax.ppermute(x, 'mp', [(0, 1), (1, 0)])  16.8 us
    pallas_call x2, Pallas kernels, mlp(): pl.pallas_call(functools.partial(mlp_kernel, approx, turned, count, first...  13 us
    unnamed x58, local copies, waits for them, and re-layouts  12 us
    pallas_call x2, Pallas kernels, project(): pl.pallas_call(functools.partial(project_kernel, count, local, turned), o...  11.2 us
    ppermute x6, starting transfers between devices, swap_mp(): return lax.ppermute(x, 'mp', [(0, 1), (1, 0)])  7.68 us
    pallas_call x2, Pallas kernels, attention(): pl.pallas_call(functools.partial(attend_kernel, local, heads), out_shape=...  6.82 us
  transfers between devices with their start and end apart: 66, of which 24 were waited for; matrix products, arithmetic and copies ran while one was open for 1% of the time, Pallas kernels for 20%

commit v1 on v0

--- a/solution.py
+++ b/solution.py
@@ -300,9 +300,9 @@
     out.wait()
 
 
-def mlp_kernel(approx, turned, count, first, table, tokens_ref, *refs):
+def raise_kernel(approx, count, first, table, tokens_ref, *refs):
     sources = refs[2 : 2 + count]
-    send_ref, hidden_ref, up, down, sent, sems = refs[2 + count :]
+    hidden_ref, up, down, sems = refs[2 + count :]
     copies = weight_copies(table, sources, first, (up, down), sems)
     for c in sum(copies, []):
         c.start()
@@ -311,7 +311,10 @@
     raise_to(approx, tokens_ref, flat(up), hidden_ref, 0, up.shape[2])
     for c in copies[1]:
         c.wait()
-    lower_other(hidden_ref, down, sent, send_ref, sems.at[2 * count], turned)
+
+
+def lower_kernel(turned, hidden_ref, down, send_ref, sent, sem):
+    lower_other(hidden_ref, down, sent, send_ref, sem.at[0], turned)
 
 
 def finish_kernel(*refs):
@@ -341,17 +344,15 @@
     )(table, *weights)
 
 
-def mlp(tokens, loaded, weights, first, table, approx, turned):
-    rows, width = tokens.shape
+def mlp_raise(tokens, loaded, weights, first, table, approx):
+    rows = tokens.shape[0]
     count = len(weights)
     shape = loaded[0].shape
-    sent = (width // 2, rows) if turned else (rows, width // 2)
     vmem = pl.BlockSpec(memory_space=pltpu.VMEM)
     anyspace = pl.BlockSpec(memory_space=pl.ANY)
-    send, hidden, _, down = pl.pallas_call(
-        functools.partial(mlp_kernel, approx, turned, count, first),
+    hidden, _, down = pl.pallas_call(
+        functools.partial(raise_kernel, approx, count, first),
         out_shape=(
-            pltpu.HBM(sent, BF16),
             pltpu.VMEM((rows, shape[2]), BF16),
             pltpu.VMEM(shape, BF16),
             pltpu.VMEM(shape, BF16),
@@ -360,16 +361,27 @@
             num_scalar_prefetch=1,
             grid=(),
             in_specs=[vmem] * 3 + [anyspace] * count,
-            out_specs=(anyspace, vmem, vmem, vmem),
-            scratch_shapes=[
-                pltpu.VMEM(sent, BF16),
-                pltpu.SemaphoreType.DMA((2 * count + 1,)),
-            ],
-        ),
-        input_output_aliases={2: 2, 3: 3},
+            out_specs=(vmem,) * 3,
+            scratch_shapes=[pltpu.SemaphoreType.DMA((max(2 * count, 1),))],
+        ),
+        input_output_aliases={2: 1, 3: 2},
         compiler_params=pltpu.CompilerParams(vmem_limit_bytes=MLP_VMEM),
     )(table, tokens, *loaded, *weights)
-    return send, hidden, down
+    return hidden, down
+
+
+def mlp_lower(hidden, down, turned):
+    rows, half = hidden.shape[0], down.shape[0] * down.shape[1] // 2
+    sent = (half, rows) if turned else (rows, half)
+    vmem = pl.BlockSpec(memory_space=pltpu.VMEM)
+    return pl.pallas_call(
+        functools.partial(lower_kernel, turned),
+        out_shape=pltpu.HBM(sent, BF16),
+        in_specs=[vmem, vmem],
+        out_specs=pl.BlockSpec(memory_space=pl.ANY),
+        scratch_shapes=[pltpu.VMEM(sent, BF16), pltpu.SemaphoreType.DMA((1,))],
+        compiler_params=pltpu.CompilerParams(vmem_limit_bytes=MLP_VMEM),
+    )(hidden, down)
 
 
 def finish(hidden_values, mids, downs):
@@ -489,7 +501,8 @@
         shards = gathered[1][e]
         first = max(len(shards) - 2, 1)
         loaded = load(shards[:first], table, seconds[e].shape[1])
-        send, hidden, down = mlp(seconds[e], loaded, shards[first:], first, table, e == 1, e == 1)
+        hidden, down = mlp_raise(seconds[e], loaded, shards[first:], first, table, e == 1)
+        send = mlp_lower(hidden, down, e == 1)
         sends.append(swap_mp(send))
         hidden_values.append(hidden)
         downs.append(down)

time: 208 us -> 202 us (0.971)
  local copies, waits for them, and re-layouts: 15.5 us -> 9.01 us
    unnamed x58 -> x38, local copies, waits for them, and re-layouts: 12 us -> 5.45 us
    pallas_call x2 -> x4, Pallas kernels: 13 us -> 12.8 us  [the longest x2 8.27 us: mlp_raise(): pl.pallas_call(functools.partial(raise_kernel, approx, count, first), out...]
  transfers between devices with their start and end apart: 66 -> 66, of which waited for: 24 -> 24; matrix products, arithmetic and copies ran while one was open for 1% -> 1% of each run, Pallas kernels for 20% -> 21%
where the time goes in v1:
time: 202 us; the launch traced here: 201 us
  waiting for transfers between devices  91 us (45%)
  starting transfers between devices  55.7 us (28%)
  Pallas kernels  41.3 us (20%)
  local copies, waits for them, and re-layouts  9.01 us (4%)
  other arithmetic  3.29 us (2%)
    ppermute x28, waiting for transfers between devices, step(): return lax.ppermute(x, 'dp', self.hop)  69.7 us
    ppermute x28, starting transfers between devices, step(): return lax.ppermute(x, 'dp', self.hop)  44.9 us
    ppermute x6, waiting for transfers between devices, swap_mp(): return lax.ppermute(x, 'mp', [(0, 1), (1, 0)])  16.8 us
    pallas_call x2, Pallas kernels, project(): pl.pallas_call(functools.partial(project_kernel, count, local, turned), o...  11.2 us
    pallas_call x2, Pallas kernels, mlp_raise(): pl.pallas_call(functools.partial(raise_kernel, approx, count, first), out...  8.27 us
    ppermute x6, starting transfers between devices, swap_mp(): return lax.ppermute(x, 'mp', [(0, 1), (1, 0)])  7.67 us
    pallas_call x2, Pallas kernels, attention(): pl.pallas_call(functools.partial(attend_kernel, local, heads), out_shape=...  6.82 us
    pallas_call x2, Pallas kernels, load(): pl.pallas_call(functools.partial(load_kernel, count), out_shape=(shape, s...  5.85 us
  transfers between devices with their start and end apart: 66, of which 24 were waited for; matrix products, arithmetic and copies ran while one was open for 1% of the time, Pallas kernels for 21%

profile of v1, /device:TPU:0, one launch (start us, length us, event | category | flops | bytes accessed | tf_op | source)
XLA Modules:
  0.0 201.4 jit_solution(6605706142082106810)
XLA Ops:
  3.6 3.0 %collective-permute-start.34 = (bf16[72,2304]{1,0:T(8,128)(2,1)S(1)}, bf16[72,2304]{1,0:T(8,128)(2,1)}, u32[]{:S(2)}, u32[]{:S(2)}) collective-permute-start(bf16[72,2304]{1,0:T(8,128)(2,1)S(1)} %concatenate.14.rest_0_), channel_id=1, source_target_pairs={{0,4},{4,12},{8,0},{12,20},{16,8},{20,28},{24,16},{28,24},{2,10},{... | collective-permute-start | bytes 995336 | tf_op jit(solution)/shard_map/ppermute | solution.py:429
  6.7 1.6 collective-permute-start.2
  9.9 4.7 %collective-permute-done.2.rest_2_ = bf16[64,2048]{1,0:T(8,128)(2,1)S(1)} collective-permute-done((bf16[64,2048]{1,0:T(8,128)(2,1)S(1)}, bf16[64,2048]{1,0:T(8,128)(2,1)S(1)}, u32[]{:S(2)}, u32[]{:S(2)}) %collective-permute-start.2) | collective-permute-done | bytes 262176 | tf_op jit(solution)/shard_map/ppermute | solution.py:429
  14.6 1.9 collective-permute-start.32
  16.5 1.5 collective-permute-start.18
  18.1 1.6 collective-permute-start.4
  20.9 7.7 %collective-permute-done.4.rest_4_ = bf16[64,2048]{1,0:T(8,128)(2,1)} collective-permute-done((bf16[64,2048]{1,0:T(8,128)(2,1)S(1)}, bf16[64,2048]{1,0:T(8,128)(2,1)}, u32[]{:S(2)}, u32[]{:S(2)}) %collective-permute-start.4) | collective-permute-done | bytes 262176 | tf_op jit(solution)/shard_map/ppermute | solution.py:429
  28.6 1.5 collective-permute-start.50
  32.2 1.6 collective-permute-start.36
  34.5 1.6 collective-permute-start.6
  36.0 6.5 %collective-permute-done.36.rest_4_ = bf16[72,2304]{1,0:T(8,128)(2,1)} collective-permute-done((bf16[72,2304]{1,0:T(8,128)(2,1)}, bf16[72,2304]{1,0:T(8,128)(2,1)}, u32[]{:S(2)}, u32[]{:S(2)}) %collective-permute-start.36) | collective-permute-done | bytes 331808 | tf_op jit(solution)/shard_map/ppermute | solution.py:429
  46.8 1.6 collective-permute-start.20
  52.7 1.5 collective-permute-done.7.rest_7_
  55.8 2.6 %collective-permute-done.20.refs_4_ = bf16[128,2048]{1,0:T(8,128)(2,1)S(1)} collective-permute-done((bf16[128,2048]{1,0:T(8,128)(2,1)}, bf16[128,2048]{1,0:T(8,128)(2,1)S(1)}, u32[]{:S(2)}, u32[]{:S(2)}) %collective-permute-start.20) | collective-permute-done | bytes 524320 | tf_op jit(solution)/shard_map/ppermute | solution.py:429
  59.9 5.2 %collective-permute-done.52.refs_4_ = bf16[144,2176]{1,0:T(8,128)(2,1)S(1)} collective-permute-done((bf16[144,2176]{1,0:T(8,128)(2,1)S(1)}, bf16[144,2176]{1,0:T(8,128)(2,1)S(1)}, u32[]{:S(2)}, u32[]{:S(2)}) %collective-permute-start.52) | collective-permute-done | bytes 626720 | tf_op jit(solution)/shard_map/ppermute | solution.py:429
  67.9 1.5 collective-permute-start.54
  69.4 7.6 %collective-permute-done.40.rest_8_ = bf16[72,2304]{1,0:T(8,128)(2,1)S(1)} collective-permute-done((bf16[72,2304]{1,0:T(8,128)(2,1)S(1)}, bf16[72,2304]{1,0:T(8,128)(2,1)S(1)}, u32[]{:S(2)}, u32[]{:S(2)}) %collective-permute-start.40) | collective-permute-done | bytes 331808 | tf_op jit(solution)/shard_map/ppermute | solution.py:429
  78.6 1.6 collective-permute-start.42
  80.6 5.9 %collective-permute-done.12.rest_12_ = bf16[64,2048]{1,0:T(8,128)(2,1)S(1)} collective-permute-done((bf16[64,2048]{1,0:T(8,128)(2,1)S(1)}, bf16[64,2048]{1,0:T(8,128)(2,1)S(1)}, u32[]{:S(2)}, u32[]{:S(2)}) %collective-permute-start.12) | collective-permute-done | bytes 262176 | tf_op jit(solution)/shard_map/ppermute | solution.py:429
  86.6 1.5 collective-permute-start.24
  88.1 2.0 %collective-permute-done.42.rest_10_ = bf16[72,2304]{1,0:T(8,128)(2,1)S(1)} collective-permute-done((bf16[72,2304]{1,0:T(8,128)(2,1)S(1)}, bf16[72,2304]{1,0:T(8,128)(2,1)S(1)}, u32[]{:S(2)}, u32[]{:S(2)}) %collective-permute-start.42) | collective-permute-done | bytes 331808 | tf_op jit(solution)/shard_map/ppermute | solution.py:429
  91.6 1.6 collective-permute-start.56
  93.2 5.3 %collective-permute-done.14.rest_14_ = bf16[64,2048]{1,0:T(8,128)(2,1)S(1)} collective-permute-done((bf16[64,2048]{1,0:T(8,128)(2,1)S(1)}, bf16[64,2048]{1,0:T(8,128)(2,1)S(1)}, u32[]{:S(2)}, u32[]{:S(2)}) %collective-permute-start.14) | collective-permute-done | bytes 262176 | tf_op jit(solution)/shard_map/ppermute | solution.py:429
  100.1 1.6 collective-permute-start.26
  101.7 7.1 %collective-permute-done.44.rest_12_ = bf16[72,2304]{1,0:T(8,128)(2,1)S(1)} collective-permute-done((bf16[72,2304]{1,0:T(8,128)(2,1)S(1)}, bf16[72,2304]{1,0:T(8,128)(2,1)S(1)}, u32[]{:S(2)}, u32[]{:S(2)}) %collective-permute-start.44) | collective-permute-done | bytes 331808 | tf_op jit(solution)/shard_map/ppermute | solution.py:429
  108.8 1.5 collective-permute-start.58
  110.4 1.6 collective-permute-start.46
  115.8 3.6 %shard_map.158 = (bf16[1024,2048]{1,0:T(8,128)(2,1)S(1)}, bf16[512,1024]{1,0:T(8,128)(2,1)S(1)}, bf16[512,1536]{1,0:T(8,128)(2,1)S(1)}) custom-call(s32[16]{0:T(128)S(1)} %dynamic-slice_bitcast_fusion.table, bf16[512,512]{1,0:T(8,128)(2,1)S(1)} %copy-done, bf16[512,512]{1,0:T(8,128)(2,1)S(1)} %copy-done.2, f32[1,1024]{1,0:T(1,128)S(1)} %bitcast.23, ...), custom_call_target="tpu_custom_call" | custom-call | tf_op jit(solution)/shard_map/pallas_call | solution.py:173
  119.5 3.0 %shard_map.159 = (f32[512,1024]{1,0:T(8,128)S(1)}, bf16[512,1024]{1,0:T(8,128)(2,1)S(1)}) custom-call(bf16[1024,2048]{1,0:T(8,128)(2,1)S(1)} %get-tuple-element.28.weight, bf16[512,1024]{1,0:T(8,128)(2,1)S(1)} %get-tuple-element.29.whole, bf16[512,1536]{1,0:T(8,128)(2,1)S(1)} %get-tuple-element.30.projected), custom_call_target="tpu_custom_call" | custom-call | tf_op jit(solution)/shard_map/pallas_call | solution.py:198
  123.1 1.6 collective-permute-start.28
  125.2 1.6 collective-permute-start.60
  127.4 4.9 %collective-permute-done.28.refs_12_ = bf16[128,2048]{1,0:T(8,128)(2,1)S(1)} collective-permute-done((bf16[128,2048]{1,0:T(8,128)(2,1)S(1)}, bf16[128,2048]{1,0:T(8,128)(2,1)S(1)}, u32[]{:S(2)}, u32[]{:S(2)}) %collective-permute-start.28) | collective-permute-done | bytes 524320 | tf_op jit(solution)/shard_map/ppermute | solution.py:429
  132.3 1.6 collective-permute-start.30
  133.9 7.6 %shard_map.163 = (bf16[1152,2304]{1,0:T(8,128)(2,1)S(1)}, bf16[512,1152]{1,0:T(8,128)(2,1)S(1)}, bf16[512,1792]{1,0:T(8,128)(2,1)S(1)}) custom-call(s32[16]{0:T(128)S(1)} %dynamic-slice_bitcast_fusion.table, bf16[576,512]{1,0:T(8,128)(2,1)} %bitcast.8.own_ref, bf16[576,512]{1,0:T(8,128)(2,1)} %collective-permute-done.32.other_ref, ...), custom_call_target="tpu_custom_call" | custom-call | tf_op jit(solution)/shard_map/pallas_call | solution.py:173
  141.5 3.8 %shard_map.164 = (f32[512,1152]{1,0:T(8,128)S(1)}, bf16[512,1152]{1,0:T(8,128)(2,1)S(1)}) custom-call(bf16[1152,2304]{1,0:T(8,128)(2,1)S(1)} %get-tuple-element.39.weight, bf16[512,1152]{1,0:T(8,128)(2,1)S(1)} %get-tuple-element.40.whole, bf16[512,1792]{1,0:T(8,128)(2,1)S(1)} %get-tuple-element.41.projected), custom_call_target="tpu_custom_call" | custom-call | tf_op jit(solution)/shard_map/pallas_call | solution.py:198
  145.3 1.6 collective-permute-start.48
  146.9 1.6 collective-permute-start.62
  152.0 5.3 %collective-permute-done.62.refs_2_ = bf16[144,2176]{1,0:T(8,128)(2,1)} collective-permute-done((bf16[144,2176]{1,0:T(8,128)(2,1)S(1)}, bf16[144,2176]{1,0:T(8,128)(2,1)}, u32[]{:S(2)}, u32[]{:S(2)}) %collective-permute-start.62) | collective-permute-done | bytes 626720 | tf_op jit(solution)/shard_map/ppermute | solution.py:429
  158.1 2.4 %shard_map.161 = (bf16[16,64,2048]{2,1,0:T(8,128)(2,1)S(1)}, bf16[16,64,2048]{2,1,0:T(8,128)(2,1)S(1)}) custom-call(s32[16]{0:T(128)S(1)} %dynamic-slice_bitcast_fusion.table, bf16[128,2048]{1,0:T(8,128)(2,1)S(1)} %pad_maximum_fusion.refs_0_, bf16[128,2048]{1,0:T(8,128)(2,1)} %collective-permute-done.17.refs_1_, ...), custom_call_target="tpu_custom_call" | custom-call | tf_op jit(solution)/shard_map/pallas_call | solution.py:333
  160.5 3.4 %shard_map.162 = (bf16[512,2048]{1,0:T(8,128)(2,1)S(1)}, bf16[16,64,2048]{2,1,0:T(8,128)(2,1)S(1)}, bf16[16,64,2048]{2,1,0:T(8,128)(2,1)S(1)}) custom-call(s32[16]{0:T(128)S(1)} %dynamic-slice_bitcast_fusion.table, bf16[512,1024]{1,0:T(8,128)(2,1)S(1)} %get-tuple-element.33.tokens_ref, ...), custom_call_target="tpu_custom_call", output_to_operand_aliasing={{1}: (2, {}), {2}: (3, {})} | custom-call | tf_op jit(solution)/shard_map/pallas_call | solution.py:353
  163.9 2.1 %shard_map.168 = bf16[512,512]{1,0:T(8,128)(2,1)} custom-call(bf16[512,2048]{1,0:T(8,128)(2,1)S(1)} %get-tuple-element.36.refs_0_.hidden_ref, bf16[16,64,2048]{2,1,0:T(8,128)(2,1)S(1)} %get-tuple-element.38.refs_2_.down), custom_call_target="tpu_custom_call" | custom-call | tf_op jit(solution)/shard_map/pallas_call | solution.py:377
  166.0 7.5 %collective-permute-done.48.got_ref = bf16[512,1152]{1,0:T(8,128)(2,1)S(1)} collective-permute-done((bf16[512,1152]{1,0:T(8,128)(2,1)S(1)}, bf16[512,1152]{1,0:T(8,128)(2,1)S(1)}, u32[]{:S(2)}, u32[]{:S(2)}) %collective-permute-start.48) | collective-permute-done | bytes 1179680 | tf_op jit(solution)/shard_map/ppermute | solution.py:401
  175.3 3.5 %shard_map.166 = (bf16[16,72,2176]{2,1,0:T(8,128)(2,1)S(1)}, bf16[16,72,2176]{2,1,0:T(8,128)(2,1)S(1)}) custom-call(s32[16]{0:T(128)S(1)} %dynamic-slice_bitcast_fusion.table, bf16[144,2176]{1,0:T(8,128)(2,1)S(1)} %fusion.2.refs_0_, bf16[144,2176]{1,0:T(8,128)(2,1)S(1)} %collective-permute-done.49.refs_1_, ...), custom_call_target="tpu_custom_call" | custom-call | tf_op jit(solution)/shard_map/pallas_call | solution.py:333
  178.8 4.9 %shard_map.167 = (bf16[512,2176]{1,0:T(8,128)(2,1)S(1)}, bf16[16,72,2176]{2,1,0:T(8,128)(2,1)S(1)}, bf16[16,72,2176]{2,1,0:T(8,128)(2,1)S(1)}) custom-call(s32[16]{0:T(128)S(1)} %dynamic-slice_bitcast_fusion.table, bf16[512,1152]{1,0:T(8,128)(2,1)S(1)} %get-tuple-element.44.tokens_ref, ...), custom_call_target="tpu_custom_call", output_to_operand_aliasing={{1}: (2, {}), {2}: (3, {})} | custom-call | tf_op jit(solution)/shard_map/pallas_call | solution.py:353
  183.7 2.4 %shard_map.169 = bf16[576,512]{1,0:T(8,128)(2,1)} custom-call(bf16[512,2176]{1,0:T(8,128)(2,1)S(1)} %get-tuple-element.47.refs_3_.hidden_ref, bf16[16,72,2176]{2,1,0:T(8,128)(2,1)S(1)} %get-tuple-element.49.refs_5_.down), custom_call_target="tpu_custom_call" | custom-call | tf_op jit(solution)/shard_map/pallas_call | solution.py:377
  186.1 1.6 collective-permute-start.65
  187.6 2.7 %finish.1 = (f32[512,512]{1,0:T(8,128)S(1)}, f32[576,512]{1,0:T(8,128)S(1)}) custom-call(bf16[512,2048]{1,0:T(8,128)(2,1)S(1)} %get-tuple-element.36.refs_0_.hidden_ref, bf16[512,512]{1,0:T(8,128)(2,1)S(1)} %get-tuple-element.37.refs_1_, bf16[16,64,2048]{2,1,0:T(8,128)(2,1)S(1)} %get-tuple-element.38.refs_2_.down, ...), custom_call_target="tpu_custom_call" | custom-call | tf_op jit(solution)/shard_map/finish/pallas_call | solution.py:390
  191.3 9.1 %collective-permute-done.65 = bf16[576,512]{1,0:T(8,128)(2,1)S(1)} collective-permute-done((bf16[576,512]{1,0:T(8,128)(2,1)}, bf16[576,512]{1,0:T(8,128)(2,1)S(1)}, u32[]{:S(2)}, u32[]{:S(2)}) %collective-permute-start.65) | collective-permute-done | bytes 589856 | tf_op jit(solution)/shard_map/ppermute | solution.py:401
  (154 shorter events, 41.7 us)
Async XLA Ops:
  3.6 14.5 %collective-permute-start.34 = (bf16[72,2304]{1,0:T(8,128)(2,1)S(1)}, bf16[72,2304]{1,0:T(8,128)(2,1)}, u32[]{:S(2)}, u32[]{:S(2)}) collective-permute-start(bf16[72,2304]{1,0:T(8,128)(2,1)S(1)} %concatenate.14.rest_0_), channel_id=1, source_target_pairs={{0,4},{4,12},{8,0},{12,20},{16,8},{20,28},{24,16},{28,24},{2,10},{... | collective-permute-start | bytes 995336 | tf_op jit(solution)/shard_map/ppermute | solution.py:429
  6.6 13.0 %collective-permute-start.33 = (bf16[72,2304]{1,0:T(8,128)(2,1)S(1)}, bf16[72,2304]{1,0:T(8,128)(2,1)S(1)}, u32[]{:S(2)}, u32[]{:S(2)}) collective-permute-start(bf16[72,2304]{1,0:T(8,128)(2,1)S(1)} %concatenate.14.rest_0_), channel_id=1, source_target_pairs={{0,2},{2,0},{4,6},{6,4},{8,10},{10,8},{12,14},{14,12},{16,18},{18,... | collective-permute-start | bytes 995336 | tf_op jit(solution)/shard_map/ppermute | solution.py:426
  8.3 22.5 %collective-permute-start = (bf16[512,512]{1,0:T(8,128)(2,1)S(1)}, bf16[512,512]{1,0:T(8,128)(2,1)S(1)}, u32[]{:S(2)}, u32[]{:S(2)}) collective-permute-start(bf16[512,512]{1,0:T(8,128)(2,1)S(1)} %copy-done), channel_id=1, source_target_pairs={{0,1},{1,0},{2,3},{3,2},{4,5},{5,4},{6,7},{7,6},{8,9},{9,8},{10,11... | collective-permute-start | bytes 1572872 | tf_op jit(solution)/shard_map/ppermute | solution.py:401
  14.6 21.4 %collective-permute-start.32 = (bf16[576,512]{1,0:T(8,128)(2,1)}, bf16[576,512]{1,0:T(8,128)(2,1)}, u32[]{:S(2)}, u32[]{:S(2)}) collective-permute-start(bf16[576,512]{1,0:T(8,128)(2,1)} %bitcast.8.own_ref), channel_id=1, source_target_pairs={{0,1},{1,0},{2,3},{3,2},{4,5},{5,4},{6,7},{7,6},{8,9},{9,8},{10,11... | collective-permute-start | bytes 1769480 | tf_op jit(solution)/shard_map/ppermute | solution.py:401
  16.5 15.6 %collective-permute-start.18 = (bf16[128,2048]{1,0:T(8,128)(2,1)S(1)}, bf16[128,2048]{1,0:T(8,128)(2,1)}, u32[]{:S(2)}, u32[]{:S(2)}) collective-permute-start(bf16[128,2048]{1,0:T(8,128)(2,1)S(1)} %pad_maximum_fusion.refs_0_), channel_id=1, source_target_pairs={{0,4},{4,12},{8,0},{12,20},{16,8},{20,28},{24,16},{28,24},{2,10},{... | collective-permute-start | bytes 1572872 | tf_op jit(solution)/shard_map/ppermute | solution.py:429
  18.1 10.6 %collective-permute-start.4 = (bf16[64,2048]{1,0:T(8,128)(2,1)S(1)}, bf16[64,2048]{1,0:T(8,128)(2,1)}, u32[]{:S(2)}, u32[]{:S(2)}) collective-permute-start(bf16[64,2048]{1,0:T(8,128)(2,1)S(1)} %collective-permute-done.2.rest_2_), channel_id=1, source_target_pairs={{0,4},{4,12},{8,0},{12,20},{16,8},{20,28},{24,16},{28,24},{2,10},{... | collective-permute-start | bytes 786440 | tf_op jit(solution)/shard_map/ppermute | solution.py:429
  19.6 10.5 %collective-permute-start.3 = (bf16[64,2048]{1,0:T(8,128)(2,1)S(1)}, bf16[64,2048]{1,0:T(8,128)(2,1)S(1)}, u32[]{:S(2)}, u32[]{:S(2)}) collective-permute-start(bf16[64,2048]{1,0:T(8,128)(2,1)S(1)} %collective-permute-done.2.rest_2_), channel_id=1, source_target_pairs={{0,2},{2,0},{4,6},{6,4},{8,10},{10,8},{12,14},{14,12},{16,18},{18,... | collective-permute-start | bytes 786440 | tf_op jit(solution)/shard_map/ppermute | solution.py:426
  28.6 15.5 %collective-permute-start.50 = (bf16[144,2176]{1,0:T(8,128)(2,1)S(1)}, bf16[144,2176]{1,0:T(8,128)(2,1)S(1)}, u32[]{:S(2)}, u32[]{:S(2)}) collective-permute-start(bf16[144,2176]{1,0:T(8,128)(2,1)S(1)} %fusion.2.refs_0_), channel_id=1, source_target_pairs={{0,4},{4,12},{8,0},{12,20},{16,8},{20,28},{24,16},{28,24},{2,10},{... | collective-permute-start | bytes 1880072 | tf_op jit(solution)/shard_map/ppermute | solution.py:429
  30.9 13.2 %collective-permute-start.49 = (bf16[144,2176]{1,0:T(8,128)(2,1)S(1)}, bf16[144,2176]{1,0:T(8,128)(2,1)S(1)}, u32[]{:S(2)}, u32[]{:S(2)}) collective-permute-start(bf16[144,2176]{1,0:T(8,128)(2,1)S(1)} %fusion.2.refs_0_), channel_id=1, source_target_pairs={{0,2},{2,0},{4,6},{6,4},{8,10},{10,8},{12,14},{14,12},{16,18},{18,... | collective-permute-start | bytes 1880072 | tf_op jit(solution)/shard_map/ppermute | solution.py:426
  32.2 10.4 %collective-permute-start.36 = (bf16[72,2304]{1,0:T(8,128)(2,1)}, bf16[72,2304]{1,0:T(8,128)(2,1)}, u32[]{:S(2)}, u32[]{:S(2)}) collective-permute-start(bf16[72,2304]{1,0:T(8,128)(2,1)} %collective-permute-done.34.rest_2_), channel_id=1, source_target_pairs={{0,4},{4,12},{8,0},{12,20},{16,8},{20,28},{24,16},{28,24},{2,10},{... | collective-permute-start | bytes 995336 | tf_op jit(solution)/shard_map/ppermute | solution.py:429
  34.5 10.8 %collective-permute-start.6 = (bf16[64,2048]{1,0:T(8,128)(2,1)}, bf16[64,2048]{1,0:T(8,128)(2,1)S(1)}, u32[]{:S(2)}, u32[]{:S(2)}) collective-permute-start(bf16[64,2048]{1,0:T(8,128)(2,1)} %collective-permute-done.4.rest_4_), channel_id=1, source_target_pairs={{0,4},{4,12},{8,0},{12,20},{16,8},{20,28},{24,16},{28,24},{2,10},{... | collective-permute-start | bytes 786440 | tf_op jit(solution)/shard_map/ppermute | solution.py:429
  36.0 10.8 %collective-permute-start.35 = (bf16[72,2304]{1,0:T(8,128)(2,1)}, bf16[72,2304]{1,0:T(8,128)(2,1)S(1)}, u32[]{:S(2)}, u32[]{:S(2)}) collective-permute-start(bf16[72,2304]{1,0:T(8,128)(2,1)} %collective-permute-done.34.rest_2_), channel_id=1, source_target_pairs={{0,2},{2,0},{4,6},{6,4},{8,10},{10,8},{12,14},{14,12},{16,18},{18,... | collective-permute-start | bytes 995336 | tf_op jit(solution)/shard_map/ppermute | solution.py:426
  46.8 11.5 %collective-permute-start.20 = (bf16[128,2048]{1,0:T(8,128)(2,1)}, bf16[128,2048]{1,0:T(8,128)(2,1)S(1)}, u32[]{:S(2)}, u32[]{:S(2)}) collective-permute-start(bf16[128,2048]{1,0:T(8,128)(2,1)} %collective-permute-done.18.refs_2_), channel_id=1, source_target_pairs={{0,4},{4,12},{8,0},{12,20},{16,8},{20,28},{24,16},{28,24},{2,10},{... | collective-permute-start | bytes 1572872 | tf_op jit(solution)/shard_map/ppermute | solution.py:429
  48.4 11.5 %collective-permute-start.19 = (bf16[128,2048]{1,0:T(8,128)(2,1)}, bf16[128,2048]{1,0:T(8,128)(2,1)S(1)}, u32[]{:S(2)}, u32[]{:S(2)}) collective-permute-start(bf16[128,2048]{1,0:T(8,128)(2,1)} %collective-permute-done.18.refs_2_), channel_id=1, source_target_pairs={{0,2},{2,0},{4,6},{6,4},{8,10},{10,8},{12,14},{14,12},{16,18},{18,... | collective-permute-start | bytes 1572872 | tf_op jit(solution)/shard_map/ppermute | solution.py:426
  49.9 15.1 %collective-permute-start.52 = (bf16[144,2176]{1,0:T(8,128)(2,1)S(1)}, bf16[144,2176]{1,0:T(8,128)(2,1)S(1)}, u32[]{:S(2)}, u32[]{:S(2)}) collective-permute-start(bf16[144,2176]{1,0:T(8,128)(2,1)S(1)} %collective-permute-done.50.refs_2_), channel_id=1, source_target_pairs={{0,4},{4,12},{8,0},{12,20},{16,8},{20,28},{24,16},{28,24},{2,10},{... | collective-permute-start | bytes 1880072 | tf_op jit(solution)/shard_map/ppermute | solution.py:429
  51.4 15.1 %collective-permute-start.51 = (bf16[144,2176]{1,0:T(8,128)(2,1)S(1)}, bf16[144,2176]{1,0:T(8,128)(2,1)S(1)}, u32[]{:S(2)}, u32[]{:S(2)}) collective-permute-start(bf16[144,2176]{1,0:T(8,128)(2,1)S(1)} %collective-permute-done.50.refs_2_), channel_id=1, source_target_pairs={{0,2},{2,0},{4,6},{6,4},{8,10},{10,8},{12,14},{14,12},{16,18},{18,... | collective-permute-start | bytes 1880072 | tf_op jit(solution)/shard_map/ppermute | solution.py:426
  54.3 13.6 %collective-permute-start.10 = (bf16[64,2048]{1,0:T(8,128)(2,1)S(1)}, bf16[64,2048]{1,0:T(8,128)(2,1)S(1)}, u32[]{:S(2)}, u32[]{:S(2)}) collective-permute-start(bf16[64,2048]{1,0:T(8,128)(2,1)S(1)} %collective-permute-done.8.rest_8_), channel_id=1, source_target_pairs={{0,4},{4,12},{8,0},{12,20},{16,8},{20,28},{24,16},{28,24},{2,10},{... | collective-permute-start | bytes 786440 | tf_op jit(solution)/shard_map/ppermute | solution.py:429
  58.3 21.8 %collective-permute-start.22 = (bf16[128,2048]{1,0:T(8,128)(2,1)S(1)}, bf16[128,2048]{1,0:T(8,128)(2,1)S(1)}, u32[]{:S(2)}, u32[]{:S(2)}) collective-permute-start(bf16[128,2048]{1,0:T(8,128)(2,1)S(1)} %collective-permute-done.20.refs_4_), channel_id=1, source_target_pairs={{0,4},{4,12},{8,0},{12,20},{16,8},{20,28},{24,16},{28,24},{2,10},{... | collective-permute-start | bytes 1572872 | tf_op jit(solution)/shard_map/ppermute | solution.py:429
  65.0 12.0 %collective-permute-start.40 = (bf16[72,2304]{1,0:T(8,128)(2,1)S(1)}, bf16[72,2304]{1,0:T(8,128)(2,1)S(1)}, u32[]{:S(2)}, u32[]{:S(2)}) collective-permute-start(bf16[72,2304]{1,0:T(8,128)(2,1)S(1)} %collective-permute-done.38.rest_6_), channel_id=1, source_target_pairs={{0,4},{4,12},{8,0},{12,20},{16,8},{20,28},{24,16},{28,24},{2,10},{... | collective-permute-start | bytes 995336 | tf_op jit(solution)/shard_map/ppermute | solution.py:429
  66.6 12.0 %collective-permute-start.39 = (bf16[72,2304]{1,0:T(8,128)(2,1)S(1)}, bf16[72,2304]{1,0:T(8,128)(2,1)S(1)}, u32[]{:S(2)}, u32[]{:S(2)}) collective-permute-start(bf16[72,2304]{1,0:T(8,128)(2,1)S(1)} %collective-permute-done.38.rest_6_), channel_id=1, source_target_pairs={{0,2},{2,0},{4,6},{6,4},{8,10},{10,8},{12,14},{14,12},{16,18},{18,... | collective-permute-start | bytes 995336 | tf_op jit(solution)/shard_map/ppermute | solution.py:426
  67.9 12.3 %collective-permute-start.21 = (bf16[128,2048]{1,0:T(8,128)(2,1)S(1)}, bf16[128,2048]{1,0:T(8,128)(2,1)S(1)}, u32[]{:S(2)}, u32[]{:S(2)}) collective-permute-start(bf16[128,2048]{1,0:T(8,128)(2,1)S(1)} %collective-permute-done.20.refs_4_), channel_id=1, source_target_pairs={{0,2},{2,0},{4,6},{6,4},{8,10},{10,8},{12,14},{14,12},{16,18},{18,... | collective-permute-start | bytes 1572872 | tf_op jit(solution)/shard_map/ppermute | solution.py:426
  67.9 23.8 %collective-permute-start.54 = (bf16[144,2176]{1,0:T(8,128)(2,1)S(1)}, bf16[144,2176]{1,0:T(8,128)(2,1)S(1)}, u32[]{:S(2)}, u32[]{:S(2)}) collective-permute-start(bf16[144,2176]{1,0:T(8,128)(2,1)S(1)} %collective-permute-done.52.refs_4_), channel_id=1, source_target_pairs={{0,4},{4,12},{8,0},{12,20},{16,8},{20,28},{24,16},{28,24},{2,10},{... | collective-permute-start | bytes 1880072 | tf_op jit(solution)/shard_map/ppermute | solution.py:429
  77.0 9.5 %collective-permute-start.12 = (bf16[64,2048]{1,0:T(8,128)(2,1)S(1)}, bf16[64,2048]{1,0:T(8,128)(2,1)S(1)}, u32[]{:S(2)}, u32[]{:S(2)}) collective-permute-start(bf16[64,2048]{1,0:T(8,128)(2,1)S(1)} %collective-permute-done.10.rest_10_), channel_id=1, source_target_pairs={{0,4},{4,12},{8,0},{12,20},{16,8},{20,28},{24,16},{28,24},{2,10},{... | collective-permute-start | bytes 786440 | tf_op jit(solution)/shard_map/ppermute | solution.py:429
  78.6 11.6 %collective-permute-start.42 = (bf16[72,2304]{1,0:T(8,128)(2,1)S(1)}, bf16[72,2304]{1,0:T(8,128)(2,1)S(1)}, u32[]{:S(2)}, u32[]{:S(2)}) collective-permute-start(bf16[72,2304]{1,0:T(8,128)(2,1)S(1)} %collective-permute-done.40.rest_8_), channel_id=1, source_target_pairs={{0,4},{4,12},{8,0},{12,20},{16,8},{20,28},{24,16},{28,24},{2,10},{... | collective-permute-start | bytes 995336 | tf_op jit(solution)/shard_map/ppermute | solution.py:429
  80.1 13.1 %collective-permute-start.41 = (bf16[72,2304]{1,0:T(8,128)(2,1)S(1)}, bf16[72,2304]{1,0:T(8,128)(2,1)S(1)}, u32[]{:S(2)}, u32[]{:S(2)}) collective-permute-start(bf16[72,2304]{1,0:T(8,128)(2,1)S(1)} %collective-permute-done.40.rest_8_), channel_id=1, source_target_pairs={{0,2},{2,0},{4,6},{6,4},{8,10},{10,8},{12,14},{14,12},{16,18},{18,... | collective-permute-start | bytes 995336 | tf_op jit(solution)/shard_map/ppermute | solution.py:426
  86.6 15.2 %collective-permute-start.53 = (bf16[144,2176]{1,0:T(8,128)(2,1)S(1)}, bf16[144,2176]{1,0:T(8,128)(2,1)S(1)}, u32[]{:S(2)}, u32[]{:S(2)}) collective-permute-start(bf16[144,2176]{1,0:T(8,128)(2,1)S(1)} %collective-permute-done.52.refs_4_), channel_id=1, source_target_pairs={{0,2},{2,0},{4,6},{6,4},{8,10},{10,8},{12,14},{14,12},{16,18},{18,... | collective-permute-start | bytes 1880072 | tf_op jit(solution)/shard_map/ppermute | solution.py:426
  86.6 13.5 %collective-permute-start.24 = (bf16[128,2048]{1,0:T(8,128)(2,1)S(1)}, bf16[128,2048]{1,0:T(8,128)(2,1)S(1)}, u32[]{:S(2)}, u32[]{:S(2)}) collective-permute-start(bf16[128,2048]{1,0:T(8,128)(2,1)S(1)} %collective-permute-done.22.refs_6_), channel_id=1, source_target_pairs={{0,4},{4,12},{8,0},{12,20},{16,8},{20,28},{24,16},{28,24},{2,10},{... | collective-permute-start | bytes 1572872 | tf_op jit(solution)/shard_map/ppermute | solution.py:429
  91.6 17.2 %collective-permute-start.56 = (bf16[144,2176]{1,0:T(8,128)(2,1)S(1)}, bf16[144,2176]{1,0:T(8,128)(2,1)S(1)}, u32[]{:S(2)}, u32[]{:S(2)}) collective-permute-start(bf16[144,2176]{1,0:T(8,128)(2,1)S(1)} %collective-permute-done.54.refs_6_), channel_id=1, source_target_pairs={{0,4},{4,12},{8,0},{12,20},{16,8},{20,28},{24,16},{28,24},{2,10},{... | collective-permute-start | bytes 1880072 | tf_op jit(solution)/shard_map/ppermute | solution.py:429
  98.6 10.3 %collective-permute-start.44 = (bf16[72,2304]{1,0:T(8,128)(2,1)S(1)}, bf16[72,2304]{1,0:T(8,128)(2,1)S(1)}, u32[]{:S(2)}, u32[]{:S(2)}) collective-permute-start(bf16[72,2304]{1,0:T(8,128)(2,1)S(1)} %collective-permute-done.42.rest_10_), channel_id=1, source_target_pairs={{0,4},{4,12},{8,0},{12,20},{16,8},{20,28},{24,16},{28,24},{2,10},{... | collective-permute-start | bytes 995336 | tf_op jit(solution)/shard_map/ppermute | solution.py:429
  100.1 22.5 %collective-permute-start.23 = (bf16[128,2048]{1,0:T(8,128)(2,1)S(1)}, bf16[128,2048]{1,0:T(8,128)(2,1)S(1)}, u32[]{:S(2)}, u32[]{:S(2)}) collective-permute-start(bf16[128,2048]{1,0:T(8,128)(2,1)S(1)} %collective-permute-done.22.refs_6_), channel_id=1, source_target_pairs={{0,2},{2,0},{4,6},{6,4},{8,10},{10,8},{12,14},{14,12},{16,18},{18,... | collective-permute-start | bytes 1572872 | tf_op jit(solution)/shard_map/ppermute | solution.py:426
  100.1 23.1 %collective-permute-start.26 = (bf16[128,2048]{1,0:T(8,128)(2,1)S(1)}, bf16[128,2048]{1,0:T(8,128)(2,1)S(1)}, u32[]{:S(2)}, u32[]{:S(2)}) collective-permute-start(bf16[128,2048]{1,0:T(8,128)(2,1)S(1)} %collective-permute-done.24.refs_8_), channel_id=1, source_target_pairs={{0,4},{4,12},{8,0},{12,20},{16,8},{20,28},{24,16},{28,24},{2,10},{... | collective-permute-start | bytes 1572872 | tf_op jit(solution)/shard_map/ppermute | solution.py:429
  108.8 16.4 %collective-permute-start.58 = (bf16[144,2176]{1,0:T(8,128)(2,1)S(1)}, bf16[144,2176]{1,0:T(8,128)(2,1)S(1)}, u32[]{:S(2)}, u32[]{:S(2)}) collective-permute-start(bf16[144,2176]{1,0:T(8,128)(2,1)S(1)} %collective-permute-done.56.refs_8_), channel_id=1, source_target_pairs={{0,4},{4,12},{8,0},{12,20},{16,8},{20,28},{24,16},{28,24},{2,10},{... | collective-permute-start | bytes 1880072 | tf_op jit(solution)/shard_map/ppermute | solution.py:429
  110.4 14.4 %collective-permute-start.46 = (bf16[72,2304]{1,0:T(8,128)(2,1)S(1)}, bf16[72,2304]{1,0:T(8,128)(2,1)S(1)}, u32[]{:S(2)}, u32[]{:S(2)}) collective-permute-start(bf16[72,2304]{1,0:T(8,128)(2,1)S(1)} %collective-permute-done.44.rest_12_), channel_id=1, source_target_pairs={{0,4},{4,12},{8,0},{12,20},{16,8},{20,28},{24,16},{28,24},{2,10},{... | collective-permute-start | bytes 995336 | tf_op jit(solution)/shard_map/ppermute | solution.py:429
  111.9 12.8 %collective-permute-start.45 = (bf16[72,2304]{1,0:T(8,128)(2,1)S(1)}, bf16[72,2304]{1,0:T(8,128)(2,1)S(1)}, u32[]{:S(2)}, u32[]{:S(2)}) collective-permute-start(bf16[72,2304]{1,0:T(8,128)(2,1)S(1)} %collective-permute-done.44.rest_12_), channel_id=1, source_target_pairs={{0,2},{2,0},{4,6},{6,4},{8,10},{10,8},{12,14},{14,12},{16,18},{18,... | collective-permute-start | bytes 995336 | tf_op jit(solution)/shard_map/ppermute | solution.py:426
  122.5 26.1 %collective-permute-start.16 = (bf16[512,1024]{1,0:T(8,128)(2,1)S(1)}, bf16[512,1024]{1,0:T(8,128)(2,1)S(1)}, u32[]{:S(2)}, u32[]{:S(2)}) collective-permute-start(bf16[512,1024]{1,0:T(8,128)(2,1)S(1)} %get-tuple-element.32), channel_id=1, source_target_pairs={{0,1},{1,0},{2,3},{3,2},{4,5},{5,4},{6,7},{7,6},{8,9},{9,8},{10,11... | collective-permute-start | bytes 3145736 | tf_op jit(solution)/shard_map/ppermute | solution.py:401
  123.1 9.2 %collective-permute-start.28 = (bf16[128,2048]{1,0:T(8,128)(2,1)S(1)}, bf16[128,2048]{1,0:T(8,128)(2,1)S(1)}, u32[]{:S(2)}, u32[]{:S(2)}) collective-permute-start(bf16[128,2048]{1,0:T(8,128)(2,1)S(1)} %collective-permute-done.26.refs_10_), channel_id=1, source_target_pairs={{0,4},{4,12},{8,0},{12,20},{16,8},{20,28},{24,16},{28,24},{2,10},{... | collective-permute-start | bytes 1572872 | tf_op jit(solution)/shard_map/ppermute | solution.py:429
  124.7 20.6 %collective-permute-start.55 = (bf16[144,2176]{1,0:T(8,128)(2,1)S(1)}, bf16[144,2176]{1,0:T(8,128)(2,1)S(1)}, u32[]{:S(2)}, u32[]{:S(2)}) collective-permute-start(bf16[144,2176]{1,0:T(8,128)(2,1)S(1)} %collective-permute-done.54.refs_6_), channel_id=1, source_target_pairs={{0,2},{2,0},{4,6},{6,4},{8,10},{10,8},{12,14},{14,12},{16,18},{18,... | collective-permute-start | bytes 1880072 | tf_op jit(solution)/shard_map/ppermute | solution.py:426
  125.2 21.6 %collective-permute-start.60 = (bf16[144,2176]{1,0:T(8,128)(2,1)S(1)}, bf16[144,2176]{1,0:T(8,128)(2,1)S(1)}, u32[]{:S(2)}, u32[]{:S(2)}) collective-permute-start(bf16[144,2176]{1,0:T(8,128)(2,1)S(1)} %collective-permute-done.58.refs_10_), channel_id=1, source_target_pairs={{0,4},{4,12},{8,0},{12,20},{16,8},{20,28},{24,16},{28,24},{2,10},{... | collective-permute-start | bytes 1880072 | tf_op jit(solution)/shard_map/ppermute | solution.py:429
  127.3 21.2 %collective-permute-start.25 = (bf16[128,2048]{1,0:T(8,128)(2,1)S(1)}, bf16[128,2048]{1,0:T(8,128)(2,1)S(1)}, u32[]{:S(2)}, u32[]{:S(2)}) collective-permute-start(bf16[128,2048]{1,0:T(8,128)(2,1)S(1)} %collective-permute-done.24.refs_8_), channel_id=1, source_target_pairs={{0,2},{2,0},{4,6},{6,4},{8,10},{10,8},{12,14},{14,12},{16,18},{18,... | collective-permute-start | bytes 1572872 | tf_op jit(solution)/shard_map/ppermute | solution.py:426
  132.3 16.6 %collective-permute-start.30 = (bf16[128,2048]{1,0:T(8,128)(2,1)S(1)}, bf16[128,2048]{1,0:T(8,128)(2,1)S(1)}, u32[]{:S(2)}, u32[]{:S(2)}) collective-permute-start(bf16[128,2048]{1,0:T(8,128)(2,1)S(1)} %collective-permute-done.28.refs_12_), channel_id=1, source_target_pairs={{0,4},{4,12},{8,0},{12,20},{16,8},{20,28},{24,16},{28,24},{2,10},{... | collective-permute-start | bytes 1572872 | tf_op jit(solution)/shard_map/ppermute | solution.py:429
  145.3 28.2 %collective-permute-start.48 = (bf16[512,1152]{1,0:T(8,128)(2,1)S(1)}, bf16[512,1152]{1,0:T(8,128)(2,1)S(1)}, u32[]{:S(2)}, u32[]{:S(2)}) collective-permute-start(bf16[512,1152]{1,0:T(8,128)(2,1)S(1)} %get-tuple-element.43), channel_id=1, source_target_pairs={{0,1},{1,0},{2,3},{3,2},{4,5},{5,4},{6,7},{7,6},{8,9},{9,8},{10,11... | collective-permute-start | bytes 3538952 | tf_op jit(solution)/shard_map/ppermute | solution.py:401
  146.9 10.4 %collective-permute-start.62 = (bf16[144,2176]{1,0:T(8,128)(2,1)S(1)}, bf16[144,2176]{1,0:T(8,128)(2,1)}, u32[]{:S(2)}, u32[]{:S(2)}) collective-permute-start(bf16[144,2176]{1,0:T(8,128)(2,1)S(1)} %collective-permute-done.60.refs_12_), channel_id=1, source_target_pairs={{0,4},{4,12},{8,0},{12,20},{16,8},{20,28},{24,16},{28,24},{2,10},{... | collective-permute-start | bytes 1880072 | tf_op jit(solution)/shard_map/ppermute | solution.py:429
  150.4 24.9 %collective-permute-start.57 = (bf16[144,2176]{1,0:T(8,128)(2,1)S(1)}, bf16[144,2176]{1,0:T(8,128)(2,1)S(1)}, u32[]{:S(2)}, u32[]{:S(2)}) collective-permute-start(bf16[144,2176]{1,0:T(8,128)(2,1)S(1)} %collective-permute-done.56.refs_8_), channel_id=1, source_target_pairs={{0,2},{2,0},{4,6},{6,4},{8,10},{10,8},{12,14},{14,12},{16,18},{18,... | collective-permute-start | bytes 1880072 | tf_op jit(solution)/shard_map/ppermute | solution.py:426
  151.1 24.2 %collective-permute-start.59 = (bf16[144,2176]{1,0:T(8,128)(2,1)S(1)}, bf16[144,2176]{1,0:T(8,128)(2,1)S(1)}, u32[]{:S(2)}, u32[]{:S(2)}) collective-permute-start(bf16[144,2176]{1,0:T(8,128)(2,1)S(1)} %collective-permute-done.58.refs_10_), channel_id=1, source_target_pairs={{0,2},{2,0},{4,6},{6,4},{8,10},{10,8},{12,14},{14,12},{16,18},{18,... | collective-permute-start | bytes 1880072 | tf_op jit(solution)/shard_map/ppermute | solution.py:426
  151.9 23.4 %collective-permute-start.61 = (bf16[144,2176]{1,0:T(8,128)(2,1)S(1)}, bf16[144,2176]{1,0:T(8,128)(2,1)S(1)}, u32[]{:S(2)}, u32[]{:S(2)}) collective-permute-start(bf16[144,2176]{1,0:T(8,128)(2,1)S(1)} %collective-permute-done.60.refs_12_), channel_id=1, source_target_pairs={{0,2},{2,0},{4,6},{6,4},{8,10},{10,8},{12,14},{14,12},{16,18},{18,... | collective-permute-start | bytes 1880072 | tf_op jit(solution)/shard_map/ppermute | solution.py:426
  157.2 21.5 %collective-permute-start.63 = (bf16[144,2176]{1,0:T(8,128)(2,1)}, bf16[144,2176]{1,0:T(8,128)(2,1)}, u32[]{:S(2)}, u32[]{:S(2)}) collective-permute-start(bf16[144,2176]{1,0:T(8,128)(2,1)} %collective-permute-done.62.refs_2_), channel_id=1, source_target_pairs={{0,2},{2,0},{4,6},{6,4},{8,10},{10,8},{12,14},{14,12},{16,18},{18,... | collective-permute-start | bytes 1880072 | tf_op jit(solution)/shard_map/ppermute | solution.py:426
  173.5 16.9 %collective-permute-start.64 = (bf16[512,512]{1,0:T(8,128)(2,1)}, bf16[512,512]{1,0:T(8,128)(2,1)S(1)}, u32[]{:S(2)}, u32[]{:S(2)}) collective-permute-start(bf16[512,512]{1,0:T(8,128)(2,1)} %shard_map.168), channel_id=1, source_target_pairs={{0,1},{1,0},{2,3},{3,2},{4,5},{5,4},{6,7},{7,6},{8,9},{9,8},{10,11... | collective-permute-start | bytes 1572872 | tf_op jit(solution)/shard_map/ppermute | solution.py:401
  186.1 14.3 %collective-permute-start.65 = (bf16[576,512]{1,0:T(8,128)(2,1)}, bf16[576,512]{1,0:T(8,128)(2,1)S(1)}, u32[]{:S(2)}, u32[]{:S(2)}) collective-permute-start(bf16[576,512]{1,0:T(8,128)(2,1)} %shard_map.169), channel_id=1, source_target_pairs={{0,1},{1,0},{2,3},{3,2},{4,5},{5,4},{6,7},{7,6},{8,9},{9,8},{10,11... | collective-permute-start | bytes 1769480 | tf_op jit(solution)/shard_map/ppermute | solution.py:401
  (37 other events, 325.9 us)
